TPU v7x, 32 devices: a whole 2x2x4 slice. The times are simulated.
32 devices in a mesh: segment: 4 (over z), space: 8 (over y, x, core).
Axes of the slice: x: 2, y: 2, z: 4, core: 2. Of those that a mesh axis runs over, the one named last changes fastest.
Arguments:
- text_states: bfloat16 [2, 8, 128, 4096], P(None, 'space'), may hold values from -6 to 6
- token_ids: int32 [2, 8, 128], replicated, may hold values from 0 to 32127, as said below
- step_ids: int32 [3, 2], replicated, may hold values from 100 to 899
- base_noise: bfloat16 [2, 8, 3, 1024], P(None, 'space'), may hold values from -6 to 6
- upscale_noise: bfloat16 [2, 8, 3, 1024], P(None, 'space'), may hold values from -6 to 6
- final_noise: bfloat16 [2, 8, 3, 512, 32], P(None, None, None, 'space'), may hold values from -6 to 6
- t5_gain: float32 [4096], replicated, may hold values from 0.5 to 1.5
- base_keyval: bfloat16 [4096, 1024], replicated, may hold values from -0.09375 to 0.09375
- upscale_keyval: bfloat16 [2, 4096, 256], replicated, may hold values from -0.09375 to 0.09375
- base_input: bfloat16 [3, 512], replicated, may hold values from -3.5 to 3.5
- base_time: bfloat16 [512, 512], replicated, may hold values from -0.25 to 0.25
- base_gain: float32 [3, 512], replicated, may hold values from 0.5 to 1.5
- base_conv: bfloat16 [9, 512, 512], replicated, may hold values from -0.09375 to 0.09375
- base_query: bfloat16 [512, 512], replicated, may hold values from -0.25 to 0.25
- base_output: bfloat16 [512, 512], replicated, may hold values from -0.25 to 0.25
- base_head: bfloat16 [512, 3], replicated, may hold values from -0.25 to 0.25
- upscale_input: bfloat16 [2, 6, 128], replicated, may hold values from -2.5 to 2.5
- upscale_time: bfloat16 [2, 128, 128], replicated, may hold values from -0.5 to 0.5
- upscale_gain: float32 [2, 3, 128], replicated, may hold values from 0.5 to 1.5
- upscale_conv: bfloat16 [2, 9, 128, 128], replicated, may hold values from -0.1875 to 0.1875
- upscale_query: bfloat16 [2, 128, 128], replicated, may hold values from -0.5 to 0.5
- upscale_output: bfloat16 [2, 128, 128], replicated, may hold values from -0.5 to 0.5
- upscale_head: bfloat16 [2, 128, 3], replicated, may hold values from -0.5 to 0.5
Outputs:
- early_states: bfloat16 [2, 2, 8, 3, 1024], P(None, None, 'space', None, 'segment')
- final_states: bfloat16 [2, 2, 8, 3, 512, 32], P(None, None, 'segment', None, 'space')
Inputs may be any that keep to these rules, and one draw needn't show every extreme that they name: `token_ids`: each prompt's ids are nonzero on its first 1 to 128 positions and 0 (padding) after them; some prompt fills all 128 positions.
All inputs are finite; a program needn't handle non-finite values.
Results may differ from a plain program's by a relative error of at most 0.0095.
Values may be sent and summed in bfloat16 or wider, within the bound.
No kernel may reach another device: no remote copies, remote signals or barrier semaphores. Data moves between devices by JAX's collectives and lax.ppermute only.
A program may use at most 256 MiB of HBM per device.

v0:
```python
import functools
import math

import jax
import jax.numpy as jnp
from jax import lax
from jax.experimental import pallas as pl
from jax.experimental.pallas import tpu as pltpu
from jax.sharding import PartitionSpec as P

HD = 64
LTXT = 128
VMEM_ALL = 67043328
LOG2E = math.log2(math.e)


NT = (((1,), (1,)), ((), ()))


def unit(x):
    return x * lax.rsqrt(jnp.sum(x * x, axis=-1, keepdims=True) * (1.0 / x.shape[-1]) + 1e-06)


def silu(x):
    return x * (0.5 + 0.5 * jnp.tanh(0.5 * x))


def fdot(a, b):
    return jnp.dot(a, b, preferred_element_type=jnp.float32)


def plane_rows(ref, at, size):
    parts = [ref[c, :, pl.ds(at, size)].astype(jnp.float32) for c in range(ref.shape[0])]
    return jnp.concatenate(parts, axis=0)


def mix_rows(rows, m, micro, total):
    zero = jnp.zeros_like(rows[0])
    out = [row if n == m else zero for row in rows for n in range(micro)]
    if total > len(out):
        out.append(jnp.zeros((total - len(out), rows[0].shape[1]), rows[0].dtype))
    return jnp.concatenate(out, axis=0)


def spread_cols(act, side, pad, dst):
    count, chans = act.shape
    pad[8 : 8 + count] = act
    col = lax.rem(lax.broadcasted_iota(jnp.int32, (count, chans), 0), side)
    left = jnp.where(col == 0, 0.0, pad[7 : 7 + count])
    right = jnp.where(col == side - 1, 0.0, pad[9 : 9 + count])
    dst[:, :chans] = left.astype(jnp.bfloat16)
    dst[:, chans : 2 * chans] = act.astype(jnp.bfloat16)
    dst[:, 2 * chans :] = right.astype(jnp.bfloat16)


def pair_keys(keys, vals):
    first = lax.broadcasted_iota(jnp.int32, keys.shape, 1) < HD
    keys, vals = keys.astype(jnp.float32), vals.astype(jnp.float32)
    kmask = jnp.concatenate([jnp.where(first, keys, 0.0), jnp.where(first, 0.0, keys)], axis=0)
    upper = jnp.concatenate([jnp.where(first, vals, 0.0), jnp.where(first, 1.0, 0.0)], axis=1)
    lower = jnp.concatenate([jnp.where(first, 0.0, vals), jnp.where(first, 0.0, 1.0)], axis=1)
    return kmask.astype(jnp.bfloat16), jnp.concatenate([upper, lower], axis=0).astype(jnp.bfloat16)


def attend_pair(query, kmask, vaug, bias):
    lanes = query.shape[1]
    half = kmask.shape[0] // 2
    scores = lax.dot_general(query, kmask, NT, preferred_element_type=jnp.float32) + bias
    probs = []
    for e in range(2):
        part = scores[:, e * half : (e + 1) * half]
        probs.append(jnp.exp2(part - jnp.max(part, axis=-1, keepdims=True)).astype(jnp.bfloat16))
    both = fdot(jnp.concatenate(probs, axis=1), vaug)
    return (both[:, :lanes] / both[:, lanes:]).astype(jnp.bfloat16)


def key_bias(ids_ref, m, who):
    bias = jnp.where(ids_ref[m, pl.ds(who, 1)] == 0, -1e30, 0.0)
    return jnp.concatenate([bias, bias], axis=1)


def back_part(h1, micro, keyvals, biases, gain1, gain2, w_query, w_out, head_rows):
    count, width = h1.shape
    each = count // micro
    query = fdot((unit(h1) * gain1).astype(jnp.bfloat16), w_query)
    query = (query * (HD**-0.5 * LOG2E)).astype(jnp.bfloat16)
    mixed = []
    for m in range(micro):
        cols = []
        for g in range(width // (2 * HD)):
            at = slice(2 * HD * g, 2 * HD * (g + 1))
            kmask, vaug = pair_keys(keyvals[m](at), keyvals[m](slice(width + at.start, width + at.stop)))
            cols.append(attend_pair(query[m * each : (m + 1) * each, at], kmask, vaug, biases[m]))
        mixed.append(jnp.concatenate(cols, axis=1) if len(cols) > 1 else cols[0])
    h2 = h1 + fdot(jnp.concatenate(mixed, axis=0), w_out)
    normed = (unit(h2) * gain2).astype(jnp.bfloat16)
    eps = 0.0
    for m in range(micro):
        rows = mix_rows(head_rows, m, micro, 16).astype(jnp.bfloat16)
        eps = eps + lax.dot_general(
            rows, normed[m * each : (m + 1) * each], NT, preferred_element_type=jnp.float32
        )
    return eps[: 3 * micro]


def alpha_bar(step):
    frac = (step / 1000.0 + 0.008) / 1.008
    return jnp.cos(frac * (math.pi / 2)) ** 2


def embed(step_ref, sec, chans):
    lane = lax.broadcasted_iota(jnp.int32, (16, chans), 1)
    row = lax.broadcasted_iota(jnp.int32, (16, chans), 0)
    half = chans // 2
    steps = jnp.zeros((16, chans), jnp.float32)
    for m in range(step_ref.shape[0]):
        steps = jnp.where(row == m, step_ref[m, sec].astype(jnp.float32), steps)
    angle = steps * jnp.exp(lax.rem(lane, half).astype(jnp.float32) * (-math.log(10000.0) / half))
    return jnp.where(lane < half, jnp.sin(angle), jnp.cos(angle)).astype(jnp.bfloat16)


def levels(step_ref, m, sec):
    step = jnp.full((8, 128), step_ref[m, sec].astype(jnp.float32))
    level, earlier = alpha_bar(step), alpha_bar(step - 50.0)
    out = (jnp.sqrt(1.0 - level), 1.0 / jnp.sqrt(level), jnp.sqrt(earlier), jnp.sqrt(1.0 - earlier))
    return [part[:1, :1] for part in out]


def denoise(noise, eps, step_ref, sec):
    micro = step_ref.shape[0]
    which = lax.rem(lax.broadcasted_iota(jnp.int32, eps.shape, 0), micro)
    table = [levels(step_ref, m, sec) for m in range(micro)]

    def scalar(n):
        out = jnp.broadcast_to(table[0][n], eps.shape)
        for m in range(1, micro):
            out = jnp.where(which == m, table[m][n], out)
        return out

    clean = jnp.clip((noise - scalar(0) * eps) * scalar(1), -1.0, 1.0)
    return clean, scalar(2) * clean + scalar(3) * eps


def begin(pairs, sems):
    copies = [pltpu.make_async_copy(src, dst, sems.at[n]) for n, (src, dst) in enumerate(pairs)]
    for copy in copies:
        copy.start()
    return copies


def front_kernel(step_ref, *refs):
    (
        text_hbm,
        t5_hbm,
        ids_hbm,
        base_x_hbm,
        first_x_hbm,
        base_in_hbm,
        base_gain_hbm,
        base_head_hbm,
        up_in_hbm,
        up_gain_hbm,
        up_head_hbm,
        up_time_hbm,
        up_conv_hbm,
        up_query_hbm,
        up_out_hbm,
        time_hbm,
        conv_hbm,
        query_hbm,
        out_hbm,
        kv_base_hbm,
        kv_up_hbm,
    ) = refs[:21]
    kv_base_out, load_out, next_out = refs[21:24]
    (
        text,
        t5_ref,
        ids_ref,
        base_x_ref,
        first_x_ref,
        base_in_ref,
        base_gain_ref,
        base_head_ref,
        up_in_ref,
        up_gain_ref,
        up_head_ref,
        up_time_ref,
        up_conv_ref,
        up_query_ref,
        up_out_ref,
        w_time,
        conv,
        w_query,
        w_out,
        kv_w,
        context,
        kv_first,
        pad_base,
        taps,
        wide_x,
        pad_first,
        cols_first,
        sems,
    ) = refs[24:]
    seg, place = lax.axis_index("segment"), lax.axis_index("space")
    segments = lax.axis_size("segment")
    rows_text, dt5 = text.shape
    micro = base_x_ref.shape[1]
    ltxt = rows_text // micro
    cb, cs = base_gain_ref.shape[1], up_gain_ref.shape[2]
    px = base_x_ref.shape[2]
    side = math.isqrt(px)
    quarter = side // 4
    band = side // segments
    bf, f32 = jnp.bfloat16, jnp.float32
    step = kv_w.shape[2]
    n_base = kv_base_hbm.shape[1] // step
    chunks = [(kv_base_hbm.at[:, n * step : (n + 1) * step], kv_w.at[n]) for n in range(n_base)]
    chunks += [(kv_up_hbm.at[n], kv_w.at[n_base + n]) for n in range(2)]
    small = (
        (ids_hbm, ids_ref),
        (base_x_hbm, base_x_ref),
        (first_x_hbm, first_x_ref),
        (base_in_hbm, base_in_ref),
        (base_gain_hbm, base_gain_ref),
        (base_head_hbm, base_head_ref),
        (up_in_hbm, up_in_ref),
        (up_gain_hbm, up_gain_ref),
        (up_head_hbm, up_head_ref),
        (up_time_hbm.at[0], up_time_ref),
        (up_conv_hbm.at[0], up_conv_ref),
        (up_query_hbm.at[0], up_query_ref),
        (up_out_hbm.at[0], up_out_ref),
        (time_hbm, w_time),
    )
    late = ((conv_hbm, conv), (query_hbm, w_query), (out_hbm, w_out))
    copies = begin([(t5_hbm, t5_ref), (text_hbm, text)] + chunks + list(small) + list(late), sems)
    after = 2 + len(chunks)

    copies[0].wait()
    copies[1].wait()
    gain = t5_ref[...]

    def prepare(i, carry):
        at = pl.multiple_of(i * 16, 16)
        x = text[pl.ds(at, 16)].astype(f32)
        context[pl.ds(at, 16)] = (unit(x) * gain).astype(bf)
        return carry

    lax.fori_loop(0, rows_text // 16, prepare, 0)
    for n in range(n_base + 2):
        copies[2 + n].wait()
        half = dt5 // 2
        out = fdot(context[:, :half], kv_w[n, :half]) + fdot(context[:, half:], kv_w[n, half:])
        out = out.astype(bf)
        if n < n_base:
            kv_base_out[:, n * step : (n + 1) * step] = out
        elif n == n_base:
            kv_first[...] = out
        else:
            load_out[: micro * ltxt] = out

    for copy in copies[after : after + len(small)]:
        copy.wait()
    biases = [key_bias(ids_ref, m, place) for m in range(micro)]

    tall = quarter + 1
    temb = fdot(embed(step_ref, 0, cb), w_time[...])
    base_rows = [base_in_ref[c : c + 1].astype(f32) for c in range(3)]
    lanes = 128 * ((tall * side + 127) // 128)
    x_t = jnp.concatenate([plane_rows(base_x_ref, 0, lanes), jnp.zeros((2, lanes), f32)], axis=0)
    x_t = jnp.transpose(x_t)[: tall * side].astype(bf)
    pad_base[: 8 + side] = jnp.zeros((8 + side, cb), f32)
    edge = lax.broadcasted_iota(jnp.int32, (quarter, cb), 0) == 0
    corner_h = []
    for m in range(micro):
        h0 = fdot(x_t, mix_rows(base_rows, m, micro, 8).astype(bf)) + temb[m : m + 1]
        pad_base[8 + side : 8 + side + tall * side] = silu(unit(h0) * base_gain_ref[0:1])
        corner_h.append(
            jnp.concatenate([h0[side * h : side * h + quarter] for h in range(quarter)], axis=0)
        )
        for r in range(quarter + 1):
            for b in range(3):
                lo = pad_base[8 + side * r + b - 1 : 8 + side * r + b - 1 + quarter]
                hi = pad_base[8 + side * (r + 1) + b - 1 : 8 + side * (r + 1) + b - 1 + quarter]
                if b == 0:
                    lo, hi = jnp.where(edge, 0.0, lo), jnp.where(edge, 0.0, hi)
                both = jnp.concatenate([lo, hi], axis=0).astype(bf)
                for a in range(3):
                    h = r - a
                    if h % 2 == 0 and 0 <= h < quarter:
                        at = m * quarter * quarter + h * quarter
                        taps[at : at + 2 * quarter, (3 * a + b) * cb : (3 * a + b + 1) * cb] = both
    copies[after + len(small)].wait()
    h1 = jnp.concatenate(corner_h, axis=0) + fdot(taps[...], conv[...])
    copies[after + len(small) + 1].wait()
    copies[after + len(small) + 2].wait()
    keyvals = [lambda at, m=m: kv_base_out[m * ltxt : (m + 1) * ltxt, at] for m in range(micro)]
    head_rows = [base_head_ref[c : c + 1].astype(f32) for c in range(3)]
    eps = back_part(
        h1, micro, keyvals, biases, base_gain_ref[1:2], base_gain_ref[2:3], w_query[...], w_out[...], head_rows
    )
    noise = plane_rows(base_x_ref, 0, lanes)
    noise = jnp.concatenate([noise[:, side * h : side * h + quarter] for h in range(quarter)], axis=1)
    corner, _ = denoise(noise, eps, step_ref, 0)

    near = 128 * ((2 * side + 127) // 128)
    window = near + band * side + near
    wide_x[...] = jnp.zeros_like(wide_x)
    wide_x[: 3 * micro, near : near + px] = plane_rows(first_x_ref, 0, px)
    x_win = wide_x[:, pl.ds(pl.multiple_of(seg * (band * side), 128), window)]
    spot = lax.broadcasted_iota(jnp.int32, (quarter * quarter, window), 0)
    pixel = lax.broadcasted_iota(jnp.int32, (quarter * quarter, window), 1) + (seg * band * side - near)
    rise = side // quarter
    hit = (lax.shift_right_arithmetic(pixel, (side * rise).bit_length() - 1) == lax.div(spot, quarter)) & (
        lax.div(lax.rem(pixel + 4 * px, side), rise) == lax.rem(spot, quarter)
    )
    corner16 = jnp.concatenate([corner, jnp.zeros((16 - 3 * micro, corner.shape[1]), f32)], axis=0).astype(bf)
    cond = fdot(corner16, jnp.where(hit, 1.0, 0.0).astype(bf))[:8]
    x_t = jnp.transpose(jnp.concatenate([x_win, cond], axis=0))
    skip = near - 2 * side
    total = (band + 4) * side
    x_t = x_t[skip : skip + total].astype(bf)
    temb = fdot(embed(step_ref, 1, cs), up_time_ref[...])
    up_rows = [up_in_ref[c, 0:1].astype(f32) for c in range(6)]
    row = lax.div(lax.broadcasted_iota(jnp.int32, (total, cs), 0), side) + (seg * band - 2)
    inside = (row >= 0) & (row < side)
    kept = (band + 2) * side
    first_h, lhs = [], []
    for m in range(micro):
        rhs = jnp.concatenate(
            [mix_rows(up_rows[:3], m, micro, 8), mix_rows(up_rows[3:], m, micro, 8)], axis=0
        ).astype(bf)
        h0 = fdot(x_t, rhs) + temb[m : m + 1]
        act = jnp.where(inside, silu(unit(h0) * up_gain_ref[0, 0:1]), 0.0)
        spread_cols(act, side, pad_first, cols_first.at[m])
        first_h.append(h0[side : side + kept])
        lhs.append(
            jnp.concatenate([cols_first[m, a * side : a * side + kept] for a in range(3)], axis=1)
        )
    h1 = jnp.concatenate(first_h, axis=0) + fdot(jnp.concatenate(lhs, axis=0), up_conv_ref[...].reshape(9 * cs, cs))
    keyvals = [lambda at, m=m: kv_first[m * ltxt : (m + 1) * ltxt, at] for m in range(micro)]
    head_rows = [up_head_ref[c, 0:1].astype(f32) for c in range(3)]
    eps = back_part(
        h1, micro, keyvals, biases, up_gain_ref[1, 0:1], up_gain_ref[2, 0:1], up_query_ref[...], up_out_ref[...],
        head_rows,
    )
    noise = x_win[: 3 * micro, near - side : near - side + kept]
    clean, prior = denoise(noise, eps, step_ref, 1)
    for c in range(3):
        next_out[c] = prior[c * micro : (c + 1) * micro, side : side + band * side].astype(bf)
    wide = load_out.shape[1]
    blocks = (load_out.shape[0] - micro * ltxt) // 16
    clean = jnp.concatenate([clean, jnp.zeros((3 * micro, blocks * wide - kept), f32)], axis=1)
    clean = jnp.concatenate([clean, jnp.zeros((16 - 3 * micro, blocks * wide), f32)], axis=0).astype(bf)
    for b in range(blocks):
        at = micro * ltxt + 16 * b
        load_out[at : at + 16] = clean[:, b * wide : (b + 1) * wide]


def base_kernel(step_ref, *refs):
    hbm, early_ref, vmem, extra = refs[:11], refs[11], refs[12:23], refs[23:]
    x_ref, w_in_ref, gain_ref, head_ref, time_ref, ids_ref, next_ref, kv_ref, conv, w_query, w_out = vmem
    wide_x, pad, cols, sems = extra
    seg, place = lax.axis_index("segment"), lax.axis_index("space")
    segments = lax.axis_size("segment")
    micro, px = x_ref.shape[1:]
    side = math.isqrt(px)
    band = side // segments
    ltxt = kv_ref.shape[0] // micro
    bf, f32 = jnp.bfloat16, jnp.float32
    copies = begin(list(zip(hbm, vmem)), sems)
    for copy in copies[:5]:
        copy.wait()
    chans = gain_ref.shape[1]
    near = 128 * ((side + 127) // 128)
    window = near + band * side + near
    wide_x[...] = jnp.zeros_like(wide_x)
    wide_x[: 3 * micro, near : near + px] = plane_rows(x_ref, 0, px)
    x_win = wide_x[:, pl.ds(pl.multiple_of(seg * (band * side), 128), window)]
    total = (band + 2) * side
    x_t = jnp.transpose(x_win)[near - side : near - side + total].astype(bf)
    temb = fdot(embed(step_ref, 0, chans), time_ref[...])
    rows = [w_in_ref[c : c + 1].astype(f32) for c in range(3)]
    row = lax.div(lax.broadcasted_iota(jnp.int32, (total, chans), 0), side) + (seg * band - 1)
    inside = (row >= 0) & (row < side)
    kept = band * side
    hid, lhs = [], []
    for m in range(micro):
        h0 = fdot(x_t, mix_rows(rows, m, micro, 8).astype(bf)) + temb[m : m + 1]
        act = jnp.where(inside, silu(unit(h0) * gain_ref[0:1]), 0.0)
        spread_cols(act, side, pad, cols.at[m])
        hid.append(h0[side : side + kept])
        lhs.append(jnp.concatenate([cols[m, a * side : a * side + kept] for a in range(3)], axis=1))
    for copy in copies[5:9]:
        copy.wait()
    h1 = jnp.concatenate(hid, axis=0) + fdot(jnp.concatenate(lhs, axis=0), conv[...])
    copies[9].wait()
    copies[10].wait()
    biases = [key_bias(ids_ref, m, place) for m in range(micro)]
    keyvals = [lambda at, m=m: kv_ref[m * ltxt : (m + 1) * ltxt, at] for m in range(micro)]
    head_rows = [head_ref[c : c + 1].astype(f32) for c in range(3)]
    eps = back_part(
        h1, micro, keyvals, biases, gain_ref[1:2], gain_ref[2:3], w_query[...], w_out[...], head_rows
    )
    _, prior = denoise(x_win[: 3 * micro, near : near + kept], eps, step_ref, 0)
    for c in range(3):
        early_ref[0, c] = prior[c * micro : (c + 1) * micro].astype(bf)
    early_ref[1] = next_ref[...]


def like(array, index=None):
    shape = array.shape if index is None else array.shape[1:]
    return pltpu.VMEM(shape, array.dtype)


def front_call(segments, steps, ids, base_x, first_x, t5, base_w, up_w, text, kv_base_w, kv_up_w):
    base_in, base_time, base_gain, base_conv, base_query, base_output, base_head = base_w
    up_in, up_time, up_gain, up_conv, up_query, up_out, up_head = up_w
    rows_text, dt5 = text.shape
    micro, px = base_x.shape[1:]
    side = math.isqrt(px)
    band = side // segments
    quarter = side // 4
    cb, cs = base_gain.shape[1], up_gain.shape[2]
    step = kv_up_w.shape[2]
    chunks = kv_base_w.shape[1] // step + 2
    near = 128 * ((2 * side + 127) // 128)
    blocks = -(-((band + 2) * side) // step)
    bf, f32 = jnp.bfloat16, jnp.float32
    smem = pl.BlockSpec(memory_space=pltpu.SMEM)
    vmem = pl.BlockSpec(memory_space=pltpu.VMEM)
    hbm = pl.BlockSpec(memory_space=pltpu.HBM)
    whole = (text, t5, ids, base_x, first_x, base_in, base_gain, base_head, up_in, up_gain, up_head)
    cut = (up_time, up_conv, up_query, up_out)
    big = (base_time, base_conv, base_query, base_output)
    args = whole + cut + big + (kv_base_w, kv_up_w)
    return pl.pallas_call(
        front_kernel,
        out_shape=(
            jax.ShapeDtypeStruct((rows_text, 2 * cb), bf),
            jax.ShapeDtypeStruct((rows_text + 16 * blocks, step), bf),
            jax.ShapeDtypeStruct((3, micro, band * side), bf),
        ),
        in_specs=[smem] + [hbm] * len(args),
        out_specs=(vmem, vmem, vmem),
        scratch_shapes=[like(a) for a in whole]
        + [like(a, 0) for a in cut]
        + [like(a) for a in big]
        + [
            pltpu.VMEM((chunks, dt5, step), bf),
            pltpu.VMEM((rows_text, dt5), bf),
            pltpu.VMEM((rows_text, step), bf),
            pltpu.VMEM((16 + side + (quarter + 1) * side, cb), f32),
            pltpu.VMEM((micro * quarter * quarter, 9 * cb), bf),
            pltpu.VMEM((8, near + px + near), f32),
            pltpu.VMEM(((band + 4) * side + 16, cs), f32),
            pltpu.VMEM((micro, (band + 4) * side, 3 * cs), bf),
            pltpu.SemaphoreType.DMA((chunks + 19,)),
        ],
        compiler_params=pltpu.CompilerParams(vmem_limit_bytes=VMEM_ALL),
        cost_estimate=pl.CostEstimate(flops=5 * 10**9, bytes_accessed=22 * 10**6, transcendentals=10**6),
        name="text_and_first",
    )(steps, *args)


def base_call(segments, steps, ids, base_x, base_w, first_next, kv_base):
    base_in, base_time, base_gain, base_conv, base_query, base_output, base_head = base_w
    micro, px = base_x.shape[1:]
    side = math.isqrt(px)
    band = side // segments
    cb = base_gain.shape[1]
    near = 128 * ((side + 127) // 128)
    bf, f32 = jnp.bfloat16, jnp.float32
    smem = pl.BlockSpec(memory_space=pltpu.SMEM)
    vmem = pl.BlockSpec(memory_space=pltpu.VMEM)
    hbm = pl.BlockSpec(memory_space=pltpu.HBM)
    args = (base_x, base_in, base_gain, base_head, base_time, ids, first_next, kv_base, base_conv, base_query)
    args += (base_output,)
    return pl.pallas_call(
        base_kernel,
        out_shape=jax.ShapeDtypeStruct((2, 3, micro, band * side), bf),
        in_specs=[smem] + [hbm] * len(args),
        out_specs=vmem,
        scratch_shapes=[like(a) for a in args]
        + [
            pltpu.VMEM((8, near + px + near), f32),
            pltpu.VMEM(((band + 2) * side + 16, cb), f32),
            pltpu.VMEM((micro, (band + 2) * side, 3 * cb), bf),
            pltpu.SemaphoreType.DMA((len(args),)),
        ],
        compiler_params=pltpu.CompilerParams(vmem_limit_bytes=VMEM_ALL),
        cost_estimate=pl.CostEstimate(flops=4 * 10**9, bytes_accessed=7 * 10**6, transcendentals=10**6),
        name="base_section",
    )(steps, *args)


def last_kernel(ratio, tall, step_ref, *refs):
    hbm, out_ref = refs[: 11 + ratio], refs[11 + ratio]
    ids_ref, mine_ref, near_ref, far_ref, w_in_ref, gain_ref, head_ref, w_time_ref, conv_ref, query_ref, out_w_ref = refs[
        12 + ratio : 23 + ratio
    ]
    load, inbig, headbig, wpair, wq2, wo2, cond_pick, act, even, odd, hid, turn, sems = refs[23 + ratio :]
    seg, place = lax.axis_index("segment"), lax.axis_index("space")
    groups = lax.axis_size("space")
    micro = step_ref.shape[0]
    span = load.shape[1] - micro * LTXT
    own = pl.ds(seg * ratio, ratio)
    pairs_io = [(hbm[4], w_in_ref), (hbm[5], gain_ref), (hbm[6], head_ref)]
    pairs_io += [(hbm[7 + n].at[1], ref) for n, ref in enumerate((w_time_ref, conv_ref, query_ref, out_w_ref))]
    pairs_io += [(hbm[0], ids_ref)]
    pairs_io += [(hbm[1 + n].at[:, own], ref) for n, ref in enumerate((mine_ref, near_ref, far_ref))]
    pairs_io += [(hbm[11 + k], load.at[k]) for k in range(ratio)]
    copies = begin(pairs_io, sems)
    chans = query_ref.shape[0]
    wide, high = mine_ref.shape[3:]
    ltxt = LTXT
    planes = 3 * wide
    phase = lax.rem(place, ratio)
    odd_place = lax.rem(place, 2) == 1
    cond_dev = high // tall
    pairs = wide // 2
    rows = high + 16
    lane2 = 2 * chans

    for copy in copies[:7]:
        copy.wait()
    row_id = lax.broadcasted_iota(jnp.int32, (2 * planes, chans), 0)
    stack = jnp.concatenate(
        [jnp.broadcast_to(w_in_ref[c, 1:2].astype(jnp.float32), (wide, chans)) for c in range(6)], axis=0
    )
    heads3 = jnp.concatenate(
        [jnp.broadcast_to(head_ref[c, 1:2].astype(jnp.float32), (wide, chans)) for c in range(3)], axis=0
    )
    for w in range(wide):
        here = lax.rem(row_id, wide) == w
        inbig[:, w * chans : (w + 1) * chans] = jnp.where(here, stack, 0.0).astype(jnp.bfloat16)
        headbig[:, w * chans : (w + 1) * chans] = jnp.where(here[:planes], heads3, 0.0).astype(jnp.bfloat16)
    zero_tap = jnp.zeros((chans, chans), jnp.bfloat16)
    for d in range(4):
        for a in range(3):
            at = (d * 3 + a) * chans
            wpair[at : at + chans, :chans] = conv_ref[3 * a + d] if d < 3 else zero_tap
            wpair[at : at + chans, chans:] = conv_ref[3 * a + d - 1] if d > 0 else zero_tap
    for dst, src in ((wq2, query_ref), (wo2, out_w_ref)):
        dst[:chans, :chans] = src[...]
        dst[:chans, chans:] = zero_tap
        dst[chans:, :chans] = zero_tap
        dst[chans:, chans:] = src[...]
    strip = cond_pick.shape[0] // 3
    pick_row = lax.broadcasted_iota(jnp.int32, (strip, planes), 0)
    pick_lane = lax.broadcasted_iota(jnp.int32, (strip, planes), 1)
    for c in range(3):
        hit = (pick_lane == c * wide + lax.rem(pick_row, wide))
        cond_pick[c * strip : (c + 1) * strip] = jnp.where(hit, 1.0, 0.0).astype(jnp.bfloat16)
    turn[...] = jnp.zeros_like(turn)
    even[0] = jnp.zeros_like(even[0])
    odd[pairs] = jnp.zeros_like(odd[pairs])

    temb = fdot(embed(step_ref, 2, chans), w_time_ref[...])
    top_ok = jnp.where(place > 0, 1.0, 0.0)
    low_ok = jnp.where(place < groups - 1, 1.0, 0.0)
    gain0, gain1, gain2 = gain_ref[0, 1:2], gain_ref[1, 1:2], gain_ref[2, 1:2]
    key_lane = lax.broadcasted_iota(jnp.int32, (ltxt, chans), 1)
    first_head = key_lane < HD
    inv = 1.0 / chans

    tile = lambda n: lax.div(lax.broadcasted_iota(jnp.int32, (lane2, lane2), n), chans)
    ones2 = jnp.where(tile(0) == tile(1), 1.0, 0.0).astype(jnp.bfloat16)
    gain0, gain1, gain2 = (jnp.concatenate([g, g], axis=1) for g in (gain0, gain1, gain2))

    def norm(x):
        total = fdot((x * x).astype(jnp.bfloat16), ones2)
        return x * lax.rsqrt(total * inv + 1e-06)

    tables = [levels(step_ref, m, 2) for m in range(micro)]
    for copy in copies[7:]:
        copy.wait()

    def image(i, carry):
        m = lax.div(i, ratio)
        k = lax.rem(i, ratio)
        r = lax.rem(phase - k + ratio, ratio)
        temb_m = jnp.where(m == 0, temb[0:1], temb[1:2])
        temb2 = jnp.concatenate([temb_m, temb_m], axis=1)

        turn[:planes, :high] = mine_ref[m, r].reshape(planes, high).astype(jnp.float32)
        body = jnp.transpose(turn[...])[:high, :planes]
        turn[:planes, :high] = near_ref[m, r].reshape(planes, high).astype(jnp.float32)
        near = jnp.transpose(turn[...])
        turn[:planes, :high] = far_ref[m, r].reshape(planes, high).astype(jnp.float32)
        far = jnp.transpose(turn[...])
        top = jnp.where(odd_place, near[high - 1 : high, :planes], far[high - 1 : high, :planes])
        low = jnp.where(odd_place, far[0:1, :planes], near[0:1, :planes])
        noise_rows = jnp.concatenate([body, top, low, jnp.zeros((14, planes), jnp.float32)], axis=0)

        blocks = [load[k, 2 * ltxt + 16 * b : 2 * ltxt + 16 * b + 8].astype(jnp.float32) for b in range(span // 16)]
        band_planes = jnp.concatenate(blocks, axis=1)[:, :strip]
        row_h = lax.broadcasted_iota(jnp.int32, (rows, strip), 0)
        lane_px = lax.broadcasted_iota(jnp.int32, (rows, strip), 1)
        need = jnp.where(
            row_h < high, 1 + lax.div(row_h, tall), jnp.where(row_h == high, 0, cond_dev + 1)
        ) + phase * cond_dev
        hit = lax.div(lane_px, wide) == need
        spread = []
        for c in range(3):
            plane = jnp.where(m == 0, band_planes[2 * c : 2 * c + 1], band_planes[2 * c + 1 : 2 * c + 2])
            spread.append(jnp.where(hit, jnp.broadcast_to(plane, (rows, strip)), 0.0).astype(jnp.bfloat16))
        cond_rows = jnp.dot(
            jnp.concatenate(spread, axis=1), cond_pick[...], preferred_element_type=jnp.float32
        )
        pixels = jnp.concatenate([noise_rows, cond_rows], axis=1).astype(jnp.bfloat16)

        def front(g, c2):
            for u in range(4):
                t = g * 4 + u
                h0 = fdot(pixels, inbig[:, pl.ds(pl.multiple_of(t * lane2, lane2), lane2)]) + temb2
                hid[t] = h0[:high]
                x = silu(norm(h0) * gain0)
                for par in range(2):
                    slot = u * 2 + par
                    at = slice(par * chans, (par + 1) * chans)
                    act[slot, 8 : 8 + high] = x[:high, at]
                    act[slot, 7:8] = x[high : high + 1, at] * top_ok
                    act[slot, 8 + high : 9 + high] = x[high + 1 : high + 2, at] * low_ok
                    wide3 = jnp.concatenate(
                        [act[slot, 7 + a : 7 + a + high].astype(jnp.bfloat16) for a in range(3)], axis=1
                    )
                    if par == 0:
                        odd[t] = wide3
                    else:
                        even[t + 1] = wide3
            return c2

        lax.fori_loop(0, pairs // 4, front, 0)

        keys = load[k, pl.ds(pl.multiple_of(m * ltxt, ltxt), ltxt), :chans].astype(jnp.float32)
        vals = load[k, pl.ds(pl.multiple_of(m * ltxt, ltxt), ltxt), chans:].astype(jnp.float32)
        ones = jnp.ones_like(keys)
        kmask = jnp.concatenate(
            [jnp.where(first_head, keys, 0.0), jnp.where(first_head, 0.0, keys)], axis=0
        ).astype(jnp.bfloat16)
        vaug = jnp.concatenate(
            [
                jnp.concatenate([jnp.where(first_head, vals, 0.0), jnp.where(first_head, ones, 0.0)], axis=1),
                jnp.concatenate([jnp.where(first_head, 0.0, vals), jnp.where(first_head, 0.0, ones)], axis=1),
            ],
            axis=0,
        ).astype(jnp.bfloat16)
        ids = ids_ref[m, pl.ds(seg * ratio + r, 1)]
        bias = jnp.where(ids == 0, -1e30, 0.0)
        bias = jnp.concatenate([bias, bias], axis=1)

        subs = 2
        each = 8
        m_rows = each * high

        def rest_of(g, c2):
            ats = [pl.multiple_of((g * subs + n) * each, each) for n in range(subs)]
            h1, q, sc, pr, mx, h2, n2 = [], [], [], [], [], [], []
            for at in ats:
                parts = [even[pl.ds(at, each)], odd[pl.ds(at, each)], even[pl.ds(at + 1, each)], odd[pl.ds(at + 1, each)]]
                lhs = jnp.concatenate([part.reshape(m_rows, 3 * chans) for part in parts], axis=1)
                h1.append(fdot(lhs, wpair[...]) + hid[pl.ds(at, each)].reshape(m_rows, lane2))
            for n in range(subs):
                qn = fdot((norm(h1[n]) * gain1).astype(jnp.bfloat16), wq2[...])
                q.append((qn * (HD**-0.5 * LOG2E)).astype(jnp.bfloat16))
            for n in range(subs):
                mixed = []
                for p in range(2):
                    scores = lax.dot_general(
                        q[n][:, p * chans : (p + 1) * chans], kmask, NT, preferred_element_type=jnp.float32
                    ) + bias
                    probs = []
                    for e in range(2):
                        s_e = scores[:, e * ltxt : (e + 1) * ltxt]
                        probs.append(jnp.exp2(s_e - jnp.max(s_e, axis=-1, keepdims=True)).astype(jnp.bfloat16))
                    both = fdot(jnp.concatenate(probs, axis=1), vaug)
                    mixed.append((both[:, :chans] / both[:, chans:]).astype(jnp.bfloat16))
                mx.append(jnp.concatenate(mixed, axis=1))
            for n in range(subs):
                h2.append(h1[n] + fdot(mx[n], wo2[...]))
            part = c2
            for n in range(subs):
                n2 = (norm(h2[n]) * gain2).astype(jnp.bfloat16).reshape(each, high, lane2)
                n2 = jnp.concatenate([n2[u] for u in range(each)], axis=1)
                at = pl.multiple_of(ats[n] * lane2, each * lane2)
                part = part + lax.dot_general(
                    headbig[:, pl.ds(at, each * lane2)], n2, NT, preferred_element_type=jnp.float32
                )
            return part

        eps = lax.fori_loop(0, pairs // (subs * each), rest_of, jnp.zeros((planes, high), jnp.float32))
        noise = mine_ref[m, r].reshape(planes, high).astype(jnp.float32)
        ca, cb, cc, cd = (jnp.where(m == 0, tables[0][n], tables[1][n]) for n in range(4))
        clean = jnp.clip((noise - ca * eps) * cb, -1.0, 1.0)
        prior = cc * clean + cd * eps
        out_ref[0, m, r] = clean.astype(jnp.bfloat16).reshape(3, wide, high)
        out_ref[1, m, r] = prior.astype(jnp.bfloat16).reshape(3, wide, high)
        return carry

    lax.fori_loop(0, micro * ratio, image, 0)


def last_call(ratio, tall, steps, ids, noise, near, far, loads, weights):
    w_in, w_time, gains, w_conv, w_query, w_out, head = weights
    micro, _, _, wide, high = noise.shape
    chans = w_query.shape[1]
    planes = 3 * wide
    pairs = wide // 2
    strip = 512
    smem = pl.BlockSpec(memory_space=pltpu.SMEM)
    vmem = pl.BlockSpec(memory_space=pltpu.VMEM)
    hbm = pl.BlockSpec(memory_space=pltpu.HBM)
    bf, f32 = jnp.bfloat16, jnp.float32
    args = (ids, noise, near, far, w_in, gains, head, w_time, w_conv, w_query, w_out) + tuple(loads)
    part = pltpu.VMEM((micro, ratio, 3, wide, high), bf)
    return pl.pallas_call(
        functools.partial(last_kernel, ratio, tall),
        out_shape=jax.ShapeDtypeStruct((2, micro, ratio, 3, wide, high), bf),
        in_specs=[smem] + [hbm] * len(args),
        out_specs=vmem,
        scratch_shapes=[like(ids), part, part, part, like(w_in), like(gains), like(head)]
        + [like(a, 0) for a in (w_time, w_conv, w_query, w_out)]
        + [
            pltpu.VMEM((ratio,) + loads[0].shape, bf),
            pltpu.VMEM((2 * planes, wide * chans), bf),
            pltpu.VMEM((planes, wide * chans), bf),
            pltpu.VMEM((12 * chans, 2 * chans), bf),
            pltpu.VMEM((2 * chans, 2 * chans), bf),
            pltpu.VMEM((2 * chans, 2 * chans), bf),
            pltpu.VMEM((3 * strip, planes), bf),
            pltpu.VMEM((8, high + 16, chans), f32),
            pltpu.VMEM((pairs + 1, high, 3 * chans), bf),
            pltpu.VMEM((pairs + 1, high, 3 * chans), bf),
            pltpu.VMEM((pairs, high, 2 * chans), f32),
            pltpu.VMEM((128, 128), f32),
            pltpu.SemaphoreType.DMA((len(args),)),
        ],
        compiler_params=pltpu.CompilerParams(vmem_limit_bytes=VMEM_ALL),
        cost_estimate=pl.CostEstimate(flops=10**10, bytes_accessed=4 * 10**6, transcendentals=10**7),
        name="last_section",
    )(steps, *args)


def shards(
    text_states,
    token_ids,
    step_ids,
    base_noise,
    upscale_noise,
    final_noise,
    t5_gain,
    base_keyval,
    upscale_keyval,
    base_input,
    base_time,
    base_gain,
    base_conv,
    base_query,
    base_output,
    base_head,
    upscale_input,
    upscale_time,
    upscale_gain,
    upscale_conv,
    upscale_query,
    upscale_output,
    upscale_head,
):
    groups = lax.axis_size("space")
    segments = lax.axis_size("segment")
    ratio = groups // segments
    micro, _, ltxt, dt5 = text_states.shape
    rows_dev, cols = final_noise.shape[3:]
    tall = rows_dev * groups // cols

    noise_t = final_noise.swapaxes(3, 4)
    swaps = [(i, i + 1) for i in range(0, groups - 1, 2)]
    near = lax.ppermute(noise_t, "space", swaps + [(j, i) for i, j in swaps])
    swaps = [(i, i + 1) for i in range(1, groups - 1, 2)]
    far = lax.ppermute(noise_t, "space", swaps + [(j, i) for i, j in swaps])

    steps = step_ids.T
    chans_base, chans_up = base_query.shape[1], upscale_query.shape[2]
    base_x = base_noise.transpose(1, 2, 0, 3)[0]
    first_x = upscale_noise.transpose(1, 2, 0, 3)[0]
    base_w = (
        base_input,
        base_time,
        base_gain,
        base_conv.reshape(9 * chans_base, chans_base),
        base_query,
        base_output,
        base_head.T,
    )
    up_in = upscale_input.transpose(1, 0, 2)
    up_gain = upscale_gain.transpose(1, 0, 2)
    up_head = upscale_head.transpose(2, 0, 1)
    up_w = (up_in, upscale_time, up_gain, upscale_conv, upscale_query, upscale_output, up_head)
    kv_base, bundle, first_next = front_call(
        segments,
        steps,
        token_ids,
        base_x,
        first_x,
        t5_gain[None],
        base_w,
        up_w,
        text_states.reshape(micro * ltxt, dt5),
        base_keyval,
        upscale_keyval,
    )
    pairs = [
        [
            (s * groups + ratio * q + r, q * groups + ratio * s + (r + k) % ratio)
            for s in range(segments)
            for q in range(segments)
            for r in range(ratio)
        ]
        for k in range(ratio)
    ]
    loads = [lax.ppermute(bundle, ("segment", "space"), pairs[k]) for k in range(ratio)]
    early = base_call(segments, steps, token_ids, base_x, base_w, first_next, kv_base)
    final = last_call(ratio, tall, steps, token_ids, noise_t, near, far, loads, up_w)
    early_states = early.transpose(0, 2, 1, 3)[:, :, None]
    return early_states, final.swapaxes(4, 5)


def solution(mesh):
    placed = (
        P(None, "space", None, None),
        P(),
        P(),
        P(None, "space", None, None),
        P(None, "space", None, None),
        P(None, None, None, "space", None),
    ) + (P(),) * 17
    return jax.shard_map(
        shards,
        mesh=mesh,
        in_specs=placed,
        out_specs=(
            P(None, None, "space", None, "segment"),
            P(None, None, "segment", None, "space", None),
        ),
        check_vma=False,
    )
```

profile of v0, /device:TPU:29, one launch (start us, length us, event | category | flops | bytes accessed | tf_op | source)
XLA Modules:
  0.0 70.9 jit_solution(15509585160860300543)
XLA Ops:
  0.6 0.7 %collective-permute-start = (bf16[2,8,3,32,64]{4,3,2,1,0:T(8,128)(2,1)}, bf16[2,8,3,32,64]{4,3,2,1,0:T(8,128)(2,1)}, u32[]{:S(2)}, u32[]{:S(2)}) collective-permute-start(bf16[2,8,3,32,64]{4,3,2,1,0:T(8,128)(2,1)} %bitcast.39), channel_id=1, source_target_pairs={{0,1},{2,3},{4,5},{6,7},{1,0},{3,2},{5,4},{7,6},{8,9},{10,11},{12,... | collective-permute-start | bytes 589832 | tf_op jit(solution)/shard_map/ppermute | solution.py:781
  1.4 3.0 %collective-permute-start.1 = (bf16[2,8,3,32,64]{4,3,2,1,0:T(8,128)(2,1)}, bf16[2,8,3,32,64]{4,3,2,1,0:T(8,128)(2,1)}, u32[]{:S(2)}, u32[]{:S(2)}) collective-permute-start(bf16[2,8,3,32,64]{4,3,2,1,0:T(8,128)(2,1)} %bitcast.40), channel_id=1, source_target_pairs={{1,2},{3,4},{5,6},{2,1},{4,3},{6,5},{9,10},{11,12},{13,14},{10,9},... | collective-permute-start | bytes 589832 | tf_op jit(solution)/shard_map/ppermute | solution.py:783
  4.4 18.6 %text_and_first.1 = (bf16[256,1024]{1,0:T(8,128)(2,1)}, bf16[288,256]{1,0:T(8,128)(2,1)}, bf16[3,2,256]{2,1,0:T(2,128)(2,1)}) custom-call(s32[2,3]{1,0:T(2,128)} %bitcast.36, bf16[256,4096]{1,0:T(8,128)(2,1)} %bitcast.23, f32[1,4096]{1,0:T(1,128)} %bitcast.24, s32[2,8,128]{2,1,0:T(8,128)} %refs_0_.1, bf16[3,2,1024]{2,1,0:T(2,128)(2,1)} %bitcast.26, ...), custom_call_target="tpu_custom_call" | custom-call | flops 5000000000 | bytes 22000000 | tf_op jit(solution)/shard_map/text_and_first/pallas_call | solution.py:439
  23.0 2.1 %collective-permute-start.2 = (bf16[288,256]{1,0:T(8,128)(2,1)}, bf16[288,256]{1,0:T(8,128)(2,1)}, u32[]{:S(2)}, u32[]{:S(2)}) collective-permute-start(bf16[288,256]{1,0:T(8,128)(2,1)} %get-tuple-element.7), channel_id=1, source_target_pairs={{0,0},{1,1},{2,8},{3,9},{4,16},{5,17},{6,24},{7,25},{8,2},{9,3},{1... | collective-permute-start | bytes 442376 | tf_op jit(solution)/shard_map/ppermute | solution.py:824
  25.2 3.0 %collective-permute-start.3 = (bf16[288,256]{1,0:T(8,128)(2,1)}, bf16[288,256]{1,0:T(8,128)(2,1)}, u32[]{:S(2)}, u32[]{:S(2)}) collective-permute-start(bf16[288,256]{1,0:T(8,128)(2,1)} %get-tuple-element.7), channel_id=1, source_target_pairs={{0,1},{1,0},{2,9},{3,8},{4,17},{5,16},{6,25},{7,24},{8,3},{9,2},{1... | collective-permute-start | bytes 442376 | tf_op jit(solution)/shard_map/ppermute | solution.py:824
  28.2 8.8 %base_section.1 = bf16[2,3,2,256]{3,2,1,0:T(2,128)(2,1)} custom-call(s32[2,3]{1,0:T(2,128)} %bitcast.37, bf16[3,2,1024]{2,1,0:T(2,128)(2,1)} %bitcast.27, bf16[3,512]{1,0:T(4,128)(2,1)} %refs_1_.1, f32[3,512]{1,0:T(4,128)} %refs_2_.3, bf16[3,512]{1,0:T(4,128)(2,1)} %bitcast.29, bf16[512,512]{1,0:T(8,128)(2,1)} %refs_4_.1, s32[2,8,128]{2,1,0:T(8,128)} %refs_0_.1, ...), custom_call_target="tpu_custom_call" | custom-call | flops 4000000000 | bytes 7000000 | tf_op jit(solution)/shard_map/base_section/pallas_call | solution.py:481
  37.0 7.0 %collective-permute-done.2.refs_11_ = bf16[288,256]{1,0:T(8,128)(2,1)} collective-permute-done((bf16[288,256]{1,0:T(8,128)(2,1)}, bf16[288,256]{1,0:T(8,128)(2,1)}, u32[]{:S(2)}, u32[]{:S(2)}) %collective-permute-start.2) | collective-permute-done | bytes 147488 | tf_op jit(solution)/shard_map/ppermute | solution.py:824
  44.0 3.5 %collective-permute-done.3.refs_12_ = bf16[288,256]{1,0:T(8,128)(2,1)} collective-permute-done((bf16[288,256]{1,0:T(8,128)(2,1)}, bf16[288,256]{1,0:T(8,128)(2,1)}, u32[]{:S(2)}, u32[]{:S(2)}) %collective-permute-start.3) | collective-permute-done | bytes 147488 | tf_op jit(solution)/shard_map/ppermute | solution.py:824
  47.5 0.0 collective-permute-done.refs_2_
  47.5 0.0 collective-permute-done.1.refs_3_
  47.5 23.2 %last_section.1 = bf16[2,2,2,3,32,64]{5,4,3,2,1,0:T(8,128)(2,1)} custom-call(s32[2,3]{1,0:T(2,128)} %bitcast.38, s32[2,8,128]{2,1,0:T(8,128)} %refs_0_.1, bf16[2,8,3,32,64]{4,3,2,1,0:T(8,128)(2,1)} %bitcast.41, bf16[2,8,3,32,64]{4,3,2,1,0:T(8,128)(2,1)} %collective-permute-done.refs_2_, bf16[2,8,3,32,64]{4,3,2,1,0:T(8,128)(2,1)} %collective-permute-done.1.refs_3_, ...), custom_call_target="tpu_custom_call" | custom-call | flops 10000000000 | bytes 4000000 | tf_op jit(solution)/shard_map/last_section/pallas_call | solution.py:719
Async XLA Ops:
  0.6 46.9 %collective-permute-start = (bf16[2,8,3,32,64]{4,3,2,1,0:T(8,128)(2,1)}, bf16[2,8,3,32,64]{4,3,2,1,0:T(8,128)(2,1)}, u32[]{:S(2)}, u32[]{:S(2)}) collective-permute-start(bf16[2,8,3,32,64]{4,3,2,1,0:T(8,128)(2,1)} %bitcast.39), channel_id=1, source_target_pairs={{0,1},{2,3},{4,5},{6,7},{1,0},{3,2},{5,4},{7,6},{8,9},{10,11},{12,... | collective-permute-start | bytes 589832 | tf_op jit(solution)/shard_map/ppermute | solution.py:781
  1.4 46.2 %collective-permute-start.1 = (bf16[2,8,3,32,64]{4,3,2,1,0:T(8,128)(2,1)}, bf16[2,8,3,32,64]{4,3,2,1,0:T(8,128)(2,1)}, u32[]{:S(2)}, u32[]{:S(2)}) collective-permute-start(bf16[2,8,3,32,64]{4,3,2,1,0:T(8,128)(2,1)} %bitcast.40), channel_id=1, source_target_pairs={{1,2},{3,4},{5,6},{2,1},{4,3},{6,5},{9,10},{11,12},{13,14},{10,9},... | collective-permute-start | bytes 589832 | tf_op jit(solution)/shard_map/ppermute | solution.py:783
  23.0 20.9 %collective-permute-start.2 = (bf16[288,256]{1,0:T(8,128)(2,1)}, bf16[288,256]{1,0:T(8,128)(2,1)}, u32[]{:S(2)}, u32[]{:S(2)}) collective-permute-start(bf16[288,256]{1,0:T(8,128)(2,1)} %get-tuple-element.7), channel_id=1, source_target_pairs={{0,0},{1,1},{2,8},{3,9},{4,16},{5,17},{6,24},{7,25},{8,2},{9,3},{1... | collective-permute-start | bytes 442376 | tf_op jit(solution)/shard_map/ppermute | solution.py:824
  25.2 22.4 %collective-permute-start.3 = (bf16[288,256]{1,0:T(8,128)(2,1)}, bf16[288,256]{1,0:T(8,128)(2,1)}, u32[]{:S(2)}, u32[]{:S(2)}) collective-permute-start(bf16[288,256]{1,0:T(8,128)(2,1)} %get-tuple-element.7), channel_id=1, source_target_pairs={{0,1},{1,0},{2,9},{3,8},{4,17},{5,16},{6,25},{7,24},{8,3},{9,2},{1... | collective-permute-start | bytes 442376 | tf_op jit(solution)/shard_map/ppermute | solution.py:824
where the time goes:
time: 71.4 us; the launch traced here: 70.9 us
  Pallas kernels  50.7 us (71%)
  waiting for transfers between devices  10.5 us (15%)
  starting transfers between devices  8.87 us (12%)
  between operations  0.83 us (1%)
    pallas_call x1, Pallas kernels, last_call(): pl.pallas_call(functools.partial(last_kernel, ratio, tall), out_shape=jax...  23.2 us
    pallas_call x1, Pallas kernels, front_call(): pl.pallas_call(front_kernel, out_shape=(jax.ShapeDtypeStruct((rows_text,...  18.6 us
    ppermute x2, waiting for transfers between devices, shards(): lax.ppermute(bundle, ('segment', 'space'), pairs[k])  10.5 us
    pallas_call x1, Pallas kernels, base_call(): pl.pallas_call(base_kernel, out_shape=jax.ShapeDtypeStruct((2, 3, micro,...  8.84 us
    ppermute x2, starting transfers between devices, shards(): lax.ppermute(bundle, ('segment', 'space'), pairs[k])  5.11 us
    ppermute x1, starting transfers between devices, shards(): far = lax.ppermute(noise_t, 'space', swaps + [(j, i) for i, j in swaps])  3.02 us
  transfers between devices with their start and end apart: 4, of which 2 were waited for; matrix products, arithmetic and copies ran while one was open for 0% of the time, Pallas kernels for 39%

commit v1 on v0

--- a/solution.py
+++ b/solution.py
@@ -7,6 +7,7 @@
 from jax.experimental import pallas as pl
 from jax.experimental.pallas import tpu as pltpu
 from jax.sharding import PartitionSpec as P
+
 
 HD = 64
 LTXT = 128
@@ -195,6 +196,7 @@
         w_out,
         kv_w,
         context,
+        scales,
         kv_first,
         pad_base,
         taps,
@@ -215,15 +217,21 @@
     band = side // segments
     bf, f32 = jnp.bfloat16, jnp.float32
     step = kv_w.shape[2]
+    half = step // 2
     n_base = kv_base_hbm.shape[1] // step
     chunks = [(kv_base_hbm.at[:, n * step : (n + 1) * step], kv_w.at[n]) for n in range(n_base)]
-    chunks += [(kv_up_hbm.at[n], kv_w.at[n_base + n]) for n in range(2)]
+    chunks += [(kv_up_hbm.at[n], kv_w.at[n_base, :, n * half : (n + 1) * half]) for n in range(2)]
+    early = (
+        (base_x_hbm, base_x_ref),
+        (base_in_hbm, base_in_ref),
+        (base_gain_hbm, base_gain_ref),
+        (time_hbm, w_time),
+        (t5_hbm, t5_ref),
+        (text_hbm, text),
+    )
     small = (
         (ids_hbm, ids_ref),
-        (base_x_hbm, base_x_ref),
         (first_x_hbm, first_x_ref),
-        (base_in_hbm, base_in_ref),
-        (base_gain_hbm, base_gain_ref),
         (base_head_hbm, base_head_ref),
         (up_in_hbm, up_in_ref),
         (up_gain_hbm, up_gain_ref),
@@ -232,39 +240,15 @@
         (up_conv_hbm.at[0], up_conv_ref),
         (up_query_hbm.at[0], up_query_ref),
         (up_out_hbm.at[0], up_out_ref),
-        (time_hbm, w_time),
     )
     late = ((conv_hbm, conv), (query_hbm, w_query), (out_hbm, w_out))
-    copies = begin([(t5_hbm, t5_ref), (text_hbm, text)] + chunks + list(small) + list(late), sems)
-    after = 2 + len(chunks)
-
-    copies[0].wait()
-    copies[1].wait()
-    gain = t5_ref[...]
-
-    def prepare(i, carry):
-        at = pl.multiple_of(i * 16, 16)
-        x = text[pl.ds(at, 16)].astype(f32)
-        context[pl.ds(at, 16)] = (unit(x) * gain).astype(bf)
-        return carry
-
-    lax.fori_loop(0, rows_text // 16, prepare, 0)
-    for n in range(n_base + 2):
-        copies[2 + n].wait()
-        half = dt5 // 2
-        out = fdot(context[:, :half], kv_w[n, :half]) + fdot(context[:, half:], kv_w[n, half:])
-        out = out.astype(bf)
-        if n < n_base:
-            kv_base_out[:, n * step : (n + 1) * step] = out
-        elif n == n_base:
-            kv_first[...] = out
-        else:
-            load_out[: micro * ltxt] = out
-
-    for copy in copies[after : after + len(small)]:
+    copies = begin(list(early) + list(small) + chunks + list(late), sems)
+    first_small = len(early)
+    first_chunk = first_small + len(small)
+    after = first_chunk + len(chunks)
+
+    for copy in copies[:4]:
         copy.wait()
-    biases = [key_bias(ids_ref, m, place) for m in range(micro)]
-
     tall = quarter + 1
     temb = fdot(embed(step_ref, 0, cb), w_time[...])
     base_rows = [base_in_ref[c : c + 1].astype(f32) for c in range(3)]
@@ -292,10 +276,36 @@
                     if h % 2 == 0 and 0 <= h < quarter:
                         at = m * quarter * quarter + h * quarter
                         taps[at : at + 2 * quarter, (3 * a + b) * cb : (3 * a + b + 1) * cb] = both
-    copies[after + len(small)].wait()
+    copies[4].wait()
+    copies[5].wait()
+    gain = t5_ref[...]
+
+    def prepare(i, carry):
+        at = pl.multiple_of(i * 16, 16)
+        x = text[pl.ds(at, 16)].astype(f32)
+        scales[pl.ds(at, 16)] = jnp.broadcast_to(
+            lax.rsqrt(jnp.sum(x * x, axis=-1, keepdims=True) * (1.0 / dt5) + 1e-06), (16, 128)
+        )
+        context[pl.ds(at, 16)] = (x * gain).astype(bf)
+        return carry
+
+    lax.fori_loop(0, rows_text // 16, prepare, 0)
+    for copy in copies[first_small:first_chunk]:
+        copy.wait()
+    biases = [key_bias(ids_ref, m, place) for m in range(micro)]
+    scale = jnp.concatenate([scales[...]] * (step // 128), axis=1)
+    for n in range(n_base):
+        copies[first_chunk + n].wait()
+        kv_base_out[:, n * step : (n + 1) * step] = (fdot(context[...], kv_w[n]) * scale).astype(bf)
+    copies[after - 2].wait()
+    copies[after - 1].wait()
+    copies[after].wait()
+    copies[after + 1].wait()
+    copies[after + 2].wait()
     h1 = jnp.concatenate(corner_h, axis=0) + fdot(taps[...], conv[...])
-    copies[after + len(small) + 1].wait()
-    copies[after + len(small) + 2].wait()
+    rest_kv = (fdot(context[...], kv_w[n_base]) * scale).astype(bf)
+    kv_first[...] = rest_kv[:, :half]
+    load_out[: micro * ltxt] = rest_kv[:, half:]
     keyvals = [lambda at, m=m: kv_base_out[m * ltxt : (m + 1) * ltxt, at] for m in range(micro)]
     head_rows = [base_head_ref[c : c + 1].astype(f32) for c in range(3)]
     eps = back_part(
@@ -449,8 +459,9 @@
         + [like(a, 0) for a in cut]
         + [like(a) for a in big]
         + [
-            pltpu.VMEM((chunks, dt5, step), bf),
+            pltpu.VMEM((chunks // 2, dt5, 2 * step), bf),
             pltpu.VMEM((rows_text, dt5), bf),
+            pltpu.VMEM((rows_text, 128), f32),
             pltpu.VMEM((rows_text, step), bf),
             pltpu.VMEM((16 + side + (quarter + 1) * side, cb), f32),
             pltpu.VMEM((micro * quarter * quarter, 9 * cb), bf),
@@ -501,7 +512,8 @@
     ids_ref, mine_ref, near_ref, far_ref, w_in_ref, gain_ref, head_ref, w_time_ref, conv_ref, query_ref, out_w_ref = refs[
         12 + ratio : 23 + ratio
     ]
-    load, inbig, headbig, wpair, wq2, wo2, cond_pick, act, even, odd, hid, turn, sems = refs[23 + ratio :]
+    load, inbig, headbig, wpair, wq2, wo2, cond_pick, act, turn, *halves, sems = refs[23 + ratio :]
+    slots = (halves[:3], halves[3:])
     seg, place = lax.axis_index("segment"), lax.axis_index("space")
     groups = lax.axis_size("space")
     micro = step_ref.shape[0]
@@ -555,15 +567,14 @@
         hit = (pick_lane == c * wide + lax.rem(pick_row, wide))
         cond_pick[c * strip : (c + 1) * strip] = jnp.where(hit, 1.0, 0.0).astype(jnp.bfloat16)
     turn[...] = jnp.zeros_like(turn)
-    even[0] = jnp.zeros_like(even[0])
-    odd[pairs] = jnp.zeros_like(odd[pairs])
+    for even, odd, _ in slots:
+        even[0] = jnp.zeros(even.shape[1:], even.dtype)
+        odd[pairs] = jnp.zeros(odd.shape[1:], odd.dtype)
 
     temb = fdot(embed(step_ref, 2, chans), w_time_ref[...])
     top_ok = jnp.where(place > 0, 1.0, 0.0)
     low_ok = jnp.where(place < groups - 1, 1.0, 0.0)
     gain0, gain1, gain2 = gain_ref[0, 1:2], gain_ref[1, 1:2], gain_ref[2, 1:2]
-    key_lane = lax.broadcasted_iota(jnp.int32, (ltxt, chans), 1)
-    first_head = key_lane < HD
     inv = 1.0 / chans
 
     tile = lambda n: lax.div(lax.broadcasted_iota(jnp.int32, (lane2, lane2), n), chans)
@@ -578,129 +589,127 @@
     for copy in copies[7:]:
         copy.wait()
 
-    def image(i, carry):
-        m = lax.div(i, ratio)
-        k = lax.rem(i, ratio)
-        r = lax.rem(phase - k + ratio, ratio)
+    def lane_norm(x):
+        return x * lax.rsqrt(jnp.sum(x * x, axis=-1, keepdims=True) * inv + 1e-06)
+
+    duos = ratio // 2
+
+    def spot(i):
+        m, k = lax.div(i, ratio), lax.rem(i, ratio)
+        duo = lax.rem(lax.div(phase, 2) - lax.rem(k, duos) + duos, duos)
+        return m, k, 2 * duo + lax.rem(phase + lax.div(k, duos), 2)
+
+    def front(i, slot):
+        even, odd, hid = slots[slot]
+        m, k, r = spot(i)
         temb_m = jnp.where(m == 0, temb[0:1], temb[1:2])
         temb2 = jnp.concatenate([temb_m, temb_m], axis=1)
 
-        turn[:planes, :high] = mine_ref[m, r].reshape(planes, high).astype(jnp.float32)
-        body = jnp.transpose(turn[...])[:high, :planes]
-        turn[:planes, :high] = near_ref[m, r].reshape(planes, high).astype(jnp.float32)
-        near = jnp.transpose(turn[...])
-        turn[:planes, :high] = far_ref[m, r].reshape(planes, high).astype(jnp.float32)
-        far = jnp.transpose(turn[...])
+        def window(ref, n):
+            turn[n, :planes, :high] = ref[m, r].reshape(planes, high).astype(jnp.float32)
+            return jnp.transpose(turn[n])
+
+        body = window(mine_ref, 0)[:high, :planes]
+        near = window(near_ref, 1)
+        far = window(far_ref, 2)
         top = jnp.where(odd_place, near[high - 1 : high, :planes], far[high - 1 : high, :planes])
         low = jnp.where(odd_place, far[0:1, :planes], near[0:1, :planes])
         noise_rows = jnp.concatenate([body, top, low, jnp.zeros((14, planes), jnp.float32)], axis=0)
-
-        blocks = [load[k, 2 * ltxt + 16 * b : 2 * ltxt + 16 * b + 8].astype(jnp.float32) for b in range(span // 16)]
+        blocks = [
+            load[k, micro * ltxt + 16 * b : micro * ltxt + 16 * b + 8].astype(jnp.float32) for b in range(span // 16)
+        ]
         band_planes = jnp.concatenate(blocks, axis=1)[:, :strip]
         row_h = lax.broadcasted_iota(jnp.int32, (rows, strip), 0)
         lane_px = lax.broadcasted_iota(jnp.int32, (rows, strip), 1)
-        need = jnp.where(
-            row_h < high, 1 + lax.div(row_h, tall), jnp.where(row_h == high, 0, cond_dev + 1)
-        ) + phase * cond_dev
-        hit = lax.div(lane_px, wide) == need
+        need = jnp.where(row_h < high, 1 + lax.div(row_h, tall), jnp.where(row_h == high, 0, cond_dev + 1))
+        hit = lax.div(lane_px, wide) == need + phase * cond_dev
         spread = []
         for c in range(3):
             plane = jnp.where(m == 0, band_planes[2 * c : 2 * c + 1], band_planes[2 * c + 1 : 2 * c + 2])
             spread.append(jnp.where(hit, jnp.broadcast_to(plane, (rows, strip)), 0.0).astype(jnp.bfloat16))
-        cond_rows = jnp.dot(
-            jnp.concatenate(spread, axis=1), cond_pick[...], preferred_element_type=jnp.float32
-        )
+        cond_rows = fdot(jnp.concatenate(spread, axis=1), cond_pick[...])
         pixels = jnp.concatenate([noise_rows, cond_rows], axis=1).astype(jnp.bfloat16)
-
-        def front(g, c2):
-            for u in range(4):
-                t = g * 4 + u
-                h0 = fdot(pixels, inbig[:, pl.ds(pl.multiple_of(t * lane2, lane2), lane2)]) + temb2
-                hid[t] = h0[:high]
-                x = silu(norm(h0) * gain0)
-                for par in range(2):
-                    slot = u * 2 + par
-                    at = slice(par * chans, (par + 1) * chans)
-                    act[slot, 8 : 8 + high] = x[:high, at]
-                    act[slot, 7:8] = x[high : high + 1, at] * top_ok
-                    act[slot, 8 + high : 9 + high] = x[high + 1 : high + 2, at] * low_ok
-                    wide3 = jnp.concatenate(
-                        [act[slot, 7 + a : 7 + a + high].astype(jnp.bfloat16) for a in range(3)], axis=1
-                    )
-                    if par == 0:
-                        odd[t] = wide3
-                    else:
-                        even[t + 1] = wide3
-            return c2
-
-        lax.fori_loop(0, pairs // 4, front, 0)
-
-        keys = load[k, pl.ds(pl.multiple_of(m * ltxt, ltxt), ltxt), :chans].astype(jnp.float32)
-        vals = load[k, pl.ds(pl.multiple_of(m * ltxt, ltxt), ltxt), chans:].astype(jnp.float32)
-        ones = jnp.ones_like(keys)
-        kmask = jnp.concatenate(
-            [jnp.where(first_head, keys, 0.0), jnp.where(first_head, 0.0, keys)], axis=0
-        ).astype(jnp.bfloat16)
-        vaug = jnp.concatenate(
-            [
-                jnp.concatenate([jnp.where(first_head, vals, 0.0), jnp.where(first_head, ones, 0.0)], axis=1),
-                jnp.concatenate([jnp.where(first_head, 0.0, vals), jnp.where(first_head, 0.0, ones)], axis=1),
-            ],
-            axis=0,
-        ).astype(jnp.bfloat16)
-        ids = ids_ref[m, pl.ds(seg * ratio + r, 1)]
-        bias = jnp.where(ids == 0, -1e30, 0.0)
-        bias = jnp.concatenate([bias, bias], axis=1)
-
-        subs = 2
-        each = 8
-        m_rows = each * high
-
-        def rest_of(g, c2):
-            ats = [pl.multiple_of((g * subs + n) * each, each) for n in range(subs)]
-            h1, q, sc, pr, mx, h2, n2 = [], [], [], [], [], [], []
-            for at in ats:
-                parts = [even[pl.ds(at, each)], odd[pl.ds(at, each)], even[pl.ds(at + 1, each)], odd[pl.ds(at + 1, each)]]
-                lhs = jnp.concatenate([part.reshape(m_rows, 3 * chans) for part in parts], axis=1)
-                h1.append(fdot(lhs, wpair[...]) + hid[pl.ds(at, each)].reshape(m_rows, lane2))
-            for n in range(subs):
-                qn = fdot((norm(h1[n]) * gain1).astype(jnp.bfloat16), wq2[...])
-                q.append((qn * (HD**-0.5 * LOG2E)).astype(jnp.bfloat16))
-            for n in range(subs):
-                mixed = []
-                for p in range(2):
-                    scores = lax.dot_general(
-                        q[n][:, p * chans : (p + 1) * chans], kmask, NT, preferred_element_type=jnp.float32
-                    ) + bias
-                    probs = []
-                    for e in range(2):
-                        s_e = scores[:, e * ltxt : (e + 1) * ltxt]
-                        probs.append(jnp.exp2(s_e - jnp.max(s_e, axis=-1, keepdims=True)).astype(jnp.bfloat16))
-                    both = fdot(jnp.concatenate(probs, axis=1), vaug)
-                    mixed.append((both[:, :chans] / both[:, chans:]).astype(jnp.bfloat16))
-                mx.append(jnp.concatenate(mixed, axis=1))
-            for n in range(subs):
-                h2.append(h1[n] + fdot(mx[n], wo2[...]))
-            part = c2
-            for n in range(subs):
-                n2 = (norm(h2[n]) * gain2).astype(jnp.bfloat16).reshape(each, high, lane2)
-                n2 = jnp.concatenate([n2[u] for u in range(each)], axis=1)
-                at = pl.multiple_of(ats[n] * lane2, each * lane2)
-                part = part + lax.dot_general(
-                    headbig[:, pl.ds(at, each * lane2)], n2, NT, preferred_element_type=jnp.float32
+        yield
+
+        for t in range(pairs):
+            h0 = fdot(pixels, inbig[:, t * lane2 : (t + 1) * lane2]) + temb2
+            hid[t] = h0[:high]
+            for par in range(2):
+                x = silu(lane_norm(h0[:, par * chans : (par + 1) * chans]) * gain0[:, :chans])
+                at = (t % 4) * 2 + par
+                act[at, 8 : 8 + high] = x[:high]
+                act[at, 7:8] = x[high : high + 1] * top_ok
+                act[at, 8 + high : 9 + high] = x[high + 1 : high + 2] * low_ok
+                wide3 = jnp.concatenate(
+                    [act[at, 7 + a : 7 + a + high].astype(jnp.bfloat16) for a in range(3)], axis=1
                 )
-            return part
-
-        eps = lax.fori_loop(0, pairs // (subs * each), rest_of, jnp.zeros((planes, high), jnp.float32))
+                if par == 0:
+                    odd[t] = wide3
+                else:
+                    even[t + 1] = wide3
+            if t % 2:
+                yield
+
+    subs = 2
+    each = pairs // subs
+    m_rows = each * high
+
+    def back(i, slot):
+        even, odd, hid = slots[slot]
+        m, k, r = spot(i)
+        keys = load[k, pl.ds(pl.multiple_of(m * ltxt, ltxt), ltxt), :chans]
+        vals = load[k, pl.ds(pl.multiple_of(m * ltxt, ltxt), ltxt), chans:]
+        kmask, vaug = pair_keys(keys, vals)
+        bias = key_bias(ids_ref, m, seg * ratio + r)
+        h1, mx = [], []
+        for n in range(subs):
+            at = n * each
+            parts = (even[at : at + each], odd[at : at + each], even[at + 1 : at + 1 + each], odd[at + 1 : at + 1 + each])
+            lhs = jnp.concatenate([part.reshape(m_rows, 3 * chans) for part in parts], axis=1)
+            h1.append(fdot(lhs, wpair[...]) + hid[at : at + each].reshape(m_rows, lane2))
+            yield
+        query = []
+        for n in range(subs):
+            qn = fdot((norm(h1[n]) * gain1).astype(jnp.bfloat16), wq2[...])
+            query.append((qn * (HD**-0.5 * LOG2E)).astype(jnp.bfloat16))
+        yield
+        for n in range(subs):
+            mixed = []
+            for p in range(2):
+                mixed.append(attend_pair(query[n][:, p * chans : (p + 1) * chans], kmask, vaug, bias))
+                yield
+            mx.append(jnp.concatenate(mixed, axis=1))
+        eps = jnp.zeros((planes, high), jnp.float32)
+        for n in range(subs):
+            h2 = h1[n] + fdot(mx[n], wo2[...])
+            rows2 = (norm(h2) * gain2).astype(jnp.bfloat16).reshape(each, high, lane2)
+            rows2 = jnp.concatenate([rows2[u] for u in range(each)], axis=1)
+            eps = eps + lax.dot_general(
+                headbig[:, n * each * lane2 : (n + 1) * each * lane2], rows2, NT, preferred_element_type=jnp.float32
+            )
+            yield
         noise = mine_ref[m, r].reshape(planes, high).astype(jnp.float32)
         ca, cb, cc, cd = (jnp.where(m == 0, tables[0][n], tables[1][n]) for n in range(4))
         clean = jnp.clip((noise - ca * eps) * cb, -1.0, 1.0)
         prior = cc * clean + cd * eps
         out_ref[0, m, r] = clean.astype(jnp.bfloat16).reshape(3, wide, high)
         out_ref[1, m, r] = prior.astype(jnp.bfloat16).reshape(3, wide, high)
+
+    def together(*streams):
+        live = list(streams)
+        while live:
+            live = [stream for stream in live if next(stream, stop) is not stop]
+
+    stop = object()
+    total = micro * ratio
+
+    def couple(j, carry):
+        together(back(2 * j, 0), front(2 * j + 1, 1))
+        together(back(2 * j + 1, 1), front(jnp.minimum(2 * j + 2, total - 1), 0))
         return carry
 
-    lax.fori_loop(0, micro * ratio, image, 0)
+    together(front(0, 0))
+    lax.fori_loop(0, total // 2, couple, 0)
 
 
 def last_call(ratio, tall, steps, ids, noise, near, far, loads, weights):
@@ -732,10 +741,15 @@
             pltpu.VMEM((2 * chans, 2 * chans), bf),
             pltpu.VMEM((3 * strip, planes), bf),
             pltpu.VMEM((8, high + 16, chans), f32),
+            pltpu.VMEM((3, 128, 128), f32),
+        ]
+        + [
             pltpu.VMEM((pairs + 1, high, 3 * chans), bf),
             pltpu.VMEM((pairs + 1, high, 3 * chans), bf),
             pltpu.VMEM((pairs, high, 2 * chans), f32),
-            pltpu.VMEM((128, 128), f32),
+        ]
+        * 2
+        + [
             pltpu.SemaphoreType.DMA((len(args),)),
         ],
         compiler_params=pltpu.CompilerParams(vmem_limit_bytes=VMEM_ALL),
@@ -783,7 +797,7 @@
     far = lax.ppermute(noise_t, "space", swaps + [(j, i) for i, j in swaps])
 
     steps = step_ids.T
-    chans_base, chans_up = base_query.shape[1], upscale_query.shape[2]
+    chans_base = base_query.shape[1]
     base_x = base_noise.transpose(1, 2, 0, 3)[0]
     first_x = upscale_noise.transpose(1, 2, 0, 3)[0]
     base_w = (
@@ -812,17 +826,21 @@
         base_keyval,
         upscale_keyval,
     )
-    pairs = [
+    duos = ratio // 2
+    cross = [
         [
-            (s * groups + ratio * q + r, q * groups + ratio * s + (r + k) % ratio)
+            (s * groups + ratio * q + r, q * groups + ratio * s + 2 * ((r // 2 + k) % duos) + r % 2)
             for s in range(segments)
             for q in range(segments)
             for r in range(ratio)
         ]
-        for k in range(ratio)
+        for k in range(duos)
     ]
-    loads = [lax.ppermute(bundle, ("segment", "space"), pairs[k]) for k in range(ratio)]
+    got = [lax.ppermute(bundle, ("segment", "space"), cross[k]) for k in range(duos)]
     early = base_call(segments, steps, token_ids, base_x, base_w, first_next, kv_base)
+    mates = [(i, i ^ 1) for i in range(groups)]
+    got, early = lax.optimization_barrier((got, early))
+    loads = got + [lax.ppermute(array, "space", mates) for array in got]
     final = last_call(ratio, tall, steps, token_ids, noise_t, near, far, loads, up_w)
     early_states = early.transpose(0, 2, 1, 3)[:, :, None]
     return early_states, final.swapaxes(4, 5)
@@ -837,6 +855,7 @@
         P(None, "space", None, None),
         P(None, None, None, "space", None),
     ) + (P(),) * 17
+
     return jax.shard_map(
         shards,
         mesh=mesh,

time: 71.4 us -> 54.6 us (0.76)
  Pallas kernels: 50.7 us -> 41.3 us
  waiting for transfers between devices: 10.5 us -> 5 us
  starting transfers between devices: 8.87 us -> 6.94 us
    ppermute x2, waiting for transfers between devices: 10.5 us -> 4.99 us  [the longest x1 3.65 us: shards(): lax.ppermute(bundle, ('segment', 'space'), cross[k])]
    pallas_call x1, Pallas kernels: 23.2 us -> 18.1 us  [last_call(): pl.pallas_call(functools.partial(last_kernel, ratio, tall), out_shape=jax...]
    pallas_call x1, Pallas kernels: 18.6 us -> 14.4 us  [front_call(): pl.pallas_call(front_kernel, out_shape=(jax.ShapeDtypeStruct((rows_text,...]
    ppermute x2, starting transfers between devices: 5.11 us -> 3.18 us  [the longest x1 2.1 us: shards(): lax.ppermute(bundle, ('segment', 'space'), cross[k])]
  transfers between devices with their start and end apart: 4 -> 4, of which waited for: 2 -> 2; matrix products, arithmetic and copies ran while one was open for 0% -> 0% of each run, Pallas kernels for 39% -> 43%
where the time goes in v1:
time: 54.6 us; the launch traced here: 54.1 us
  Pallas kernels  41.3 us (76%)
  starting transfers between devices  6.94 us (13%)
  waiting for transfers between devices  5 us (9%)
  between operations  0.85 us (2%)
    pallas_call x1, Pallas kernels, last_call(): pl.pallas_call(functools.partial(last_kernel, ratio, tall), out_shape=jax...  18.1 us
    pallas_call x1, Pallas kernels, front_call(): pl.pallas_call(front_kernel, out_shape=(jax.ShapeDtypeStruct((rows_text,...  14.4 us
    pallas_call x1, Pallas kernels, base_call(): pl.pallas_call(base_kernel, out_shape=jax.ShapeDtypeStruct((2, 3, micro,...  8.85 us
    ppermute x1, waiting for transfers between devices, shards(): lax.ppermute(bundle, ('segment', 'space'), cross[k])  3.65 us
    ppermute x1, starting transfers between devices, shards(): far = lax.ppermute(noise_t, 'space', swaps + [(j, i) for i, j in swaps])  3.02 us
    ppermute x1, starting transfers between devices, shards(): lax.ppermute(bundle, ('segment', 'space'), cross[k])  2.1 us
    ppermute x1, waiting for transfers between devices, shards(): loads = got + [lax.ppermute(array, 'space', mates) for array in got]  1.34 us
  transfers between devices with their start and end apart: 4, of which 2 were waited for; matrix products, arithmetic and copies ran while one was open for 0% of the time, Pallas kernels for 43%

profile of v1, /device:TPU:29, one launch (start us, length us, event | category | flops | bytes accessed | tf_op | source)
XLA Modules:
  0.0 54.1 jit_solution(7393070287253969461)
XLA Ops:
  0.6 0.7 %collective-permute-start.1 = (bf16[2,8,3,32,64]{4,3,2,1,0:T(8,128)(2,1)}, bf16[2,8,3,32,64]{4,3,2,1,0:T(8,128)(2,1)}, u32[]{:S(2)}, u32[]{:S(2)}) collective-permute-start(bf16[2,8,3,32,64]{4,3,2,1,0:T(8,128)(2,1)} %bitcast.39), channel_id=1, source_target_pairs={{0,1},{2,3},{4,5},{6,7},{1,0},{3,2},{5,4},{7,6},{8,9},{10,11},{12,... | collective-permute-start | bytes 589832 | tf_op jit(solution)/shard_map/ppermute | solution.py:795
  1.4 3.0 %collective-permute-start.2 = (bf16[2,8,3,32,64]{4,3,2,1,0:T(8,128)(2,1)}, bf16[2,8,3,32,64]{4,3,2,1,0:T(8,128)(2,1)}, u32[]{:S(2)}, u32[]{:S(2)}) collective-permute-start(bf16[2,8,3,32,64]{4,3,2,1,0:T(8,128)(2,1)} %bitcast.40), channel_id=1, source_target_pairs={{1,2},{3,4},{5,6},{2,1},{4,3},{6,5},{9,10},{11,12},{13,14},{10,9},... | collective-permute-start | bytes 589832 | tf_op jit(solution)/shard_map/ppermute | solution.py:797
  4.4 14.4 %text_and_first.1 = (bf16[256,1024]{1,0:T(8,128)(2,1)}, bf16[288,256]{1,0:T(8,128)(2,1)}, bf16[3,2,256]{2,1,0:T(2,128)(2,1)}) custom-call(s32[2,3]{1,0:T(2,128)} %bitcast.36, bf16[256,4096]{1,0:T(8,128)(2,1)} %bitcast.23, f32[1,4096]{1,0:T(1,128)} %bitcast.24, s32[2,8,128]{2,1,0:T(8,128)} %refs_0_.1, bf16[3,2,1024]{2,1,0:T(2,128)(2,1)} %bitcast.26, ...), custom_call_target="tpu_custom_call" | custom-call | flops 5000000000 | bytes 22000000 | tf_op jit(solution)/shard_map/text_and_first/pallas_call | solution.py:449
  18.8 2.1 %collective-permute-start = (bf16[288,256]{1,0:T(8,128)(2,1)}, bf16[288,256]{1,0:T(8,128)(2,1)}, u32[]{:S(2)}, u32[]{:S(2)}) collective-permute-start(bf16[288,256]{1,0:T(8,128)(2,1)} %get-tuple-element.7), channel_id=1, source_target_pairs={{0,0},{1,1},{2,8},{3,9},{4,16},{5,17},{6,24},{7,25},{8,2},{9,3},{1... | collective-permute-start | bytes 442376 | tf_op jit(solution)/shard_map/ppermute | solution.py:839
  20.9 8.8 %base_section.1 = bf16[2,3,2,256]{3,2,1,0:T(2,128)(2,1)} custom-call(s32[2,3]{1,0:T(2,128)} %bitcast.37, bf16[3,2,1024]{2,1,0:T(2,128)(2,1)} %bitcast.27, bf16[3,512]{1,0:T(4,128)(2,1)} %refs_1_.1, f32[3,512]{1,0:T(4,128)} %refs_2_.3, bf16[3,512]{1,0:T(4,128)(2,1)} %bitcast.29, bf16[512,512]{1,0:T(8,128)(2,1)} %refs_4_.1, s32[2,8,128]{2,1,0:T(8,128)} %refs_0_.1, ...), custom_call_target="tpu_custom_call" | custom-call | flops 4000000000 | bytes 7000000 | tf_op jit(solution)/shard_map/base_section/pallas_call | solution.py:492
  29.7 3.7 %collective-permute-done.refs_11_ = bf16[288,256]{1,0:T(8,128)(2,1)} collective-permute-done((bf16[288,256]{1,0:T(8,128)(2,1)}, bf16[288,256]{1,0:T(8,128)(2,1)}, u32[]{:S(2)}, u32[]{:S(2)}) %collective-permute-start) | collective-permute-done | bytes 147488 | tf_op jit(solution)/shard_map/ppermute | solution.py:839
  33.4 1.1 %collective-permute-start.3 = (bf16[288,256]{1,0:T(8,128)(2,1)}, bf16[288,256]{1,0:T(8,128)(2,1)}, u32[]{:S(2)}, u32[]{:S(2)}) collective-permute-start(bf16[288,256]{1,0:T(8,128)(2,1)} %collective-permute-done.refs_11_), channel_id=1, source_target_pairs={{0,1},{1,0},{2,3},{3,2},{4,5},{5,4},{6,7},{7,6},{8,9},{9,8},{10,11... | collective-permute-start | bytes 442376 | tf_op jit(solution)/shard_map/ppermute | solution.py:843
  34.5 0.0 collective-permute-done.1.refs_2_
  34.5 0.0 collective-permute-done.2.refs_3_
  34.5 1.3 %collective-permute-done.3.refs_12_ = bf16[288,256]{1,0:T(8,128)(2,1)} collective-permute-done((bf16[288,256]{1,0:T(8,128)(2,1)}, bf16[288,256]{1,0:T(8,128)(2,1)}, u32[]{:S(2)}, u32[]{:S(2)}) %collective-permute-start.3) | collective-permute-done | bytes 147488 | tf_op jit(solution)/shard_map/ppermute | solution.py:843
  35.8 18.1 %last_section.1 = bf16[2,2,2,3,32,64]{5,4,3,2,1,0:T(8,128)(2,1)} custom-call(s32[2,3]{1,0:T(2,128)} %bitcast.38, s32[2,8,128]{2,1,0:T(8,128)} %refs_0_.1, bf16[2,8,3,32,64]{4,3,2,1,0:T(8,128)(2,1)} %bitcast.41, bf16[2,8,3,32,64]{4,3,2,1,0:T(8,128)(2,1)} %collective-permute-done.1.refs_2_, bf16[2,8,3,32,64]{4,3,2,1,0:T(8,128)(2,1)} %collective-permute-done.2.refs_3_, ...), custom_call_target="tpu_custom_call" | custom-call | flops 10000000000 | bytes 4000000 | tf_op jit(solution)/shard_map/last_section/pallas_call | solution.py:728
Async XLA Ops:
  0.6 33.8 %collective-permute-start.1 = (bf16[2,8,3,32,64]{4,3,2,1,0:T(8,128)(2,1)}, bf16[2,8,3,32,64]{4,3,2,1,0:T(8,128)(2,1)}, u32[]{:S(2)}, u32[]{:S(2)}) collective-permute-start(bf16[2,8,3,32,64]{4,3,2,1,0:T(8,128)(2,1)} %bitcast.39), channel_id=1, source_target_pairs={{0,1},{2,3},{4,5},{6,7},{1,0},{3,2},{5,4},{7,6},{8,9},{10,11},{12,... | collective-permute-start | bytes 589832 | tf_op jit(solution)/shard_map/ppermute | solution.py:795
  1.4 33.1 %collective-permute-start.2 = (bf16[2,8,3,32,64]{4,3,2,1,0:T(8,128)(2,1)}, bf16[2,8,3,32,64]{4,3,2,1,0:T(8,128)(2,1)}, u32[]{:S(2)}, u32[]{:S(2)}) collective-permute-start(bf16[2,8,3,32,64]{4,3,2,1,0:T(8,128)(2,1)} %bitcast.40), channel_id=1, source_target_pairs={{1,2},{3,4},{5,6},{2,1},{4,3},{6,5},{9,10},{11,12},{13,14},{10,9},... | collective-permute-start | bytes 589832 | tf_op jit(solution)/shard_map/ppermute | solution.py:797
  18.8 14.6 %collective-permute-start = (bf16[288,256]{1,0:T(8,128)(2,1)}, bf16[288,256]{1,0:T(8,128)(2,1)}, u32[]{:S(2)}, u32[]{:S(2)}) collective-permute-start(bf16[288,256]{1,0:T(8,128)(2,1)} %get-tuple-element.7), channel_id=1, source_target_pairs={{0,0},{1,1},{2,8},{3,9},{4,16},{5,17},{6,24},{7,25},{8,2},{9,3},{1... | collective-permute-start | bytes 442376 | tf_op jit(solution)/shard_map/ppermute | solution.py:839
  33.4 2.4 %collective-permute-start.3 = (bf16[288,256]{1,0:T(8,128)(2,1)}, bf16[288,256]{1,0:T(8,128)(2,1)}, u32[]{:S(2)}, u32[]{:S(2)}) collective-permute-start(bf16[288,256]{1,0:T(8,128)(2,1)} %collective-permute-done.refs_11_), channel_id=1, source_target_pairs={{0,1},{1,0},{2,3},{3,2},{4,5},{5,4},{6,7},{7,6},{8,9},{9,8},{10,11... | collective-permute-start | bytes 442376 | tf_op jit(solution)/shard_map/ppermute | solution.py:843

commit v2 on v1

--- a/solution.py
+++ b/solution.py
@@ -46,12 +46,20 @@
 def spread_cols(act, side, pad, dst):
     count, chans = act.shape
     pad[8 : 8 + count] = act
-    col = lax.rem(lax.broadcasted_iota(jnp.int32, (count, chans), 0), side)
-    left = jnp.where(col == 0, 0.0, pad[7 : 7 + count])
-    right = jnp.where(col == side - 1, 0.0, pad[9 : 9 + count])
+    col = lax.broadcasted_iota(jnp.int32, (1, side, chans), 1)
+    left = pad[7 : 7 + count].reshape(count // side, side, chans)
+    right = pad[9 : 9 + count].reshape(count // side, side, chans)
+    left = jnp.where(col == 0, 0.0, left).reshape(count, chans)
+    right = jnp.where(col == side - 1, 0.0, right).reshape(count, chans)
     dst[:, :chans] = left.astype(jnp.bfloat16)
     dst[:, chans : 2 * chans] = act.astype(jnp.bfloat16)
     dst[:, 2 * chans :] = right.astype(jnp.bfloat16)
+
+
+def inside_only(act, outer, seg, segments):
+    top = act[:outer] * jnp.where(seg > 0, 1.0, 0.0)
+    low = act[act.shape[0] - outer :] * jnp.where(seg < segments - 1, 1.0, 0.0)
+    return jnp.concatenate([top, act[outer : act.shape[0] - outer], low], axis=0)
 
 
 def pair_keys(keys, vals):
@@ -172,8 +180,9 @@
         out_hbm,
         kv_base_hbm,
         kv_up_hbm,
-    ) = refs[:21]
-    kv_base_out, load_out, next_out = refs[21:24]
+        noise_hbm,
+    ) = refs[:22]
+    kv_base_out, load_out, next_out, mine_out = refs[22:26]
     (
         text,
         t5_ref,
@@ -204,7 +213,7 @@
         pad_first,
         cols_first,
         sems,
-    ) = refs[24:]
+    ) = refs[26:]
     seg, place = lax.axis_index("segment"), lax.axis_index("space")
     segments = lax.axis_size("segment")
     rows_text, dt5 = text.shape
@@ -241,11 +250,13 @@
         (up_query_hbm.at[0], up_query_ref),
         (up_out_hbm.at[0], up_out_ref),
     )
+    ratio = mine_out.shape[1]
     late = ((conv_hbm, conv), (query_hbm, w_query), (out_hbm, w_out))
-    copies = begin(list(early) + list(small) + chunks + list(late), sems)
+    late += ((noise_hbm.at[:, pl.ds(seg * ratio, ratio)], mine_out),)
+    copies = begin(list(early) + list(small) + chunks[:n_base] + list(late[:3]) + chunks[n_base:] + list(late[3:]), sems)
     first_small = len(early)
     first_chunk = first_small + len(small)
-    after = first_chunk + len(chunks)
+    after = first_chunk + n_base
 
     for copy in copies[:4]:
         copy.wait()
@@ -280,16 +291,22 @@
     copies[5].wait()
     gain = t5_ref[...]
 
+    lump = 512
+
     def prepare(i, carry):
         at = pl.multiple_of(i * 16, 16)
-        x = text[pl.ds(at, 16)].astype(f32)
-        scales[pl.ds(at, 16)] = jnp.broadcast_to(
-            lax.rsqrt(jnp.sum(x * x, axis=-1, keepdims=True) * (1.0 / dt5) + 1e-06), (16, 128)
-        )
-        context[pl.ds(at, 16)] = (x * gain).astype(bf)
+        sums = jnp.zeros((16, 128), f32)
+        for c in range(0, dt5, lump):
+            x = text[pl.ds(at, 16), c : c + lump].astype(f32)
+            square = x * x
+            for n in range(0, lump, 128):
+                sums = sums + square[:, n : n + 128]
+            context[pl.ds(at, 16), c : c + lump] = (x * gain[:, c : c + lump]).astype(bf)
+        mean = jnp.sum(sums, axis=-1, keepdims=True) * (1.0 / dt5)
+        scales[pl.ds(at, 16)] = jnp.broadcast_to(lax.rsqrt(mean + 1e-06), (16, 128))
         return carry
 
-    lax.fori_loop(0, rows_text // 16, prepare, 0)
+    lax.fori_loop(0, rows_text // 16, prepare, 0, unroll=2)
     for copy in copies[first_small:first_chunk]:
         copy.wait()
     biases = [key_bias(ids_ref, m, place) for m in range(micro)]
@@ -297,15 +314,10 @@
     for n in range(n_base):
         copies[first_chunk + n].wait()
         kv_base_out[:, n * step : (n + 1) * step] = (fdot(context[...], kv_w[n]) * scale).astype(bf)
-    copies[after - 2].wait()
-    copies[after - 1].wait()
     copies[after].wait()
+    h1 = jnp.concatenate(corner_h, axis=0) + fdot(taps[...], conv[...])
     copies[after + 1].wait()
     copies[after + 2].wait()
-    h1 = jnp.concatenate(corner_h, axis=0) + fdot(taps[...], conv[...])
-    rest_kv = (fdot(context[...], kv_w[n_base]) * scale).astype(bf)
-    kv_first[...] = rest_kv[:, :half]
-    load_out[: micro * ltxt] = rest_kv[:, half:]
     keyvals = [lambda at, m=m: kv_base_out[m * ltxt : (m + 1) * ltxt, at] for m in range(micro)]
     head_rows = [base_head_ref[c : c + 1].astype(f32) for c in range(3)]
     eps = back_part(
@@ -315,6 +327,11 @@
     noise = jnp.concatenate([noise[:, side * h : side * h + quarter] for h in range(quarter)], axis=1)
     corner, _ = denoise(noise, eps, step_ref, 0)
 
+    for copy in copies[after + 3 :]:
+        copy.wait()
+    rest_kv = (fdot(context[...], kv_w[n_base]) * scale).astype(bf)
+    kv_first[...] = rest_kv[:, :half]
+    load_out[: micro * ltxt] = rest_kv[:, half:]
     near = 128 * ((2 * side + 127) // 128)
     window = near + band * side + near
     wide_x[...] = jnp.zeros_like(wide_x)
@@ -334,8 +351,6 @@
     x_t = x_t[skip : skip + total].astype(bf)
     temb = fdot(embed(step_ref, 1, cs), up_time_ref[...])
     up_rows = [up_in_ref[c, 0:1].astype(f32) for c in range(6)]
-    row = lax.div(lax.broadcasted_iota(jnp.int32, (total, cs), 0), side) + (seg * band - 2)
-    inside = (row >= 0) & (row < side)
     kept = (band + 2) * side
     first_h, lhs = [], []
     for m in range(micro):
@@ -343,7 +358,7 @@
             [mix_rows(up_rows[:3], m, micro, 8), mix_rows(up_rows[3:], m, micro, 8)], axis=0
         ).astype(bf)
         h0 = fdot(x_t, rhs) + temb[m : m + 1]
-        act = jnp.where(inside, silu(unit(h0) * up_gain_ref[0, 0:1]), 0.0)
+        act = inside_only(silu(unit(h0) * up_gain_ref[0, 0:1]), 2 * side, seg, segments)
         spread_cols(act, side, pad_first, cols_first.at[m])
         first_h.append(h0[side : side + kept])
         lhs.append(
@@ -371,7 +386,7 @@
 
 def base_kernel(step_ref, *refs):
     hbm, early_ref, vmem, extra = refs[:11], refs[11], refs[12:23], refs[23:]
-    x_ref, w_in_ref, gain_ref, head_ref, time_ref, ids_ref, next_ref, kv_ref, conv, w_query, w_out = vmem
+    x_ref, w_in_ref, gain_ref, head_ref, time_ref, conv, ids_ref, next_ref, kv_ref, w_query, w_out = vmem
     wide_x, pad, cols, sems = extra
     seg, place = lax.axis_index("segment"), lax.axis_index("space")
     segments = lax.axis_size("segment")
@@ -393,21 +408,18 @@
     x_t = jnp.transpose(x_win)[near - side : near - side + total].astype(bf)
     temb = fdot(embed(step_ref, 0, chans), time_ref[...])
     rows = [w_in_ref[c : c + 1].astype(f32) for c in range(3)]
-    row = lax.div(lax.broadcasted_iota(jnp.int32, (total, chans), 0), side) + (seg * band - 1)
-    inside = (row >= 0) & (row < side)
     kept = band * side
     hid, lhs = [], []
     for m in range(micro):
         h0 = fdot(x_t, mix_rows(rows, m, micro, 8).astype(bf)) + temb[m : m + 1]
-        act = jnp.where(inside, silu(unit(h0) * gain_ref[0:1]), 0.0)
+        act = inside_only(silu(unit(h0) * gain_ref[0:1]), side, seg, segments)
         spread_cols(act, side, pad, cols.at[m])
         hid.append(h0[side : side + kept])
         lhs.append(jnp.concatenate([cols[m, a * side : a * side + kept] for a in range(3)], axis=1))
-    for copy in copies[5:9]:
+    copies[5].wait()
+    h1 = jnp.concatenate(hid, axis=0) + fdot(jnp.concatenate(lhs, axis=0), conv[...])
+    for copy in copies[6:]:
         copy.wait()
-    h1 = jnp.concatenate(hid, axis=0) + fdot(jnp.concatenate(lhs, axis=0), conv[...])
-    copies[9].wait()
-    copies[10].wait()
     biases = [key_bias(ids_ref, m, place) for m in range(micro)]
     keyvals = [lambda at, m=m: kv_ref[m * ltxt : (m + 1) * ltxt, at] for m in range(micro)]
     head_rows = [head_ref[c : c + 1].astype(f32) for c in range(3)]
@@ -425,7 +437,7 @@
     return pltpu.VMEM(shape, array.dtype)
 
 
-def front_call(segments, steps, ids, base_x, first_x, t5, base_w, up_w, text, kv_base_w, kv_up_w):
+def front_call(segments, steps, ids, base_x, first_x, t5, base_w, up_w, text, kv_base_w, kv_up_w, noise, ratio):
     base_in, base_time, base_gain, base_conv, base_query, base_output, base_head = base_w
     up_in, up_time, up_gain, up_conv, up_query, up_out, up_head = up_w
     rows_text, dt5 = text.shape
@@ -445,16 +457,17 @@
     whole = (text, t5, ids, base_x, first_x, base_in, base_gain, base_head, up_in, up_gain, up_head)
     cut = (up_time, up_conv, up_query, up_out)
     big = (base_time, base_conv, base_query, base_output)
-    args = whole + cut + big + (kv_base_w, kv_up_w)
+    args = whole + cut + big + (kv_base_w, kv_up_w, noise)
     return pl.pallas_call(
         front_kernel,
         out_shape=(
             jax.ShapeDtypeStruct((rows_text, 2 * cb), bf),
             jax.ShapeDtypeStruct((rows_text + 16 * blocks, step), bf),
             jax.ShapeDtypeStruct((3, micro, band * side), bf),
+            jax.ShapeDtypeStruct(noise.shape[:1] + (ratio,) + noise.shape[2:], bf),
         ),
         in_specs=[smem] + [hbm] * len(args),
-        out_specs=(vmem, vmem, vmem),
+        out_specs=(vmem, vmem, vmem, vmem),
         scratch_shapes=[like(a) for a in whole]
         + [like(a, 0) for a in cut]
         + [like(a) for a in big]
@@ -468,7 +481,7 @@
             pltpu.VMEM((8, near + px + near), f32),
             pltpu.VMEM(((band + 4) * side + 16, cs), f32),
             pltpu.VMEM((micro, (band + 4) * side, 3 * cs), bf),
-            pltpu.SemaphoreType.DMA((chunks + 19,)),
+            pltpu.SemaphoreType.DMA((chunks + 20,)),
         ],
         compiler_params=pltpu.CompilerParams(vmem_limit_bytes=VMEM_ALL),
         cost_estimate=pl.CostEstimate(flops=5 * 10**9, bytes_accessed=22 * 10**6, transcendentals=10**6),
@@ -487,7 +500,7 @@
     smem = pl.BlockSpec(memory_space=pltpu.SMEM)
     vmem = pl.BlockSpec(memory_space=pltpu.VMEM)
     hbm = pl.BlockSpec(memory_space=pltpu.HBM)
-    args = (base_x, base_in, base_gain, base_head, base_time, ids, first_next, kv_base, base_conv, base_query)
+    args = (base_x, base_in, base_gain, base_head, base_time, base_conv, ids, first_next, kv_base, base_query)
     args += (base_output,)
     return pl.pallas_call(
         base_kernel,
@@ -518,11 +531,10 @@
     groups = lax.axis_size("space")
     micro = step_ref.shape[0]
     span = load.shape[1] - micro * LTXT
-    own = pl.ds(seg * ratio, ratio)
     pairs_io = [(hbm[4], w_in_ref), (hbm[5], gain_ref), (hbm[6], head_ref)]
     pairs_io += [(hbm[7 + n].at[1], ref) for n, ref in enumerate((w_time_ref, conv_ref, query_ref, out_w_ref))]
     pairs_io += [(hbm[0], ids_ref)]
-    pairs_io += [(hbm[1 + n].at[:, own], ref) for n, ref in enumerate((mine_ref, near_ref, far_ref))]
+    pairs_io += [(hbm[1 + n], ref) for n, ref in enumerate((mine_ref, near_ref, far_ref))]
     pairs_io += [(hbm[11 + k], load.at[k]) for k in range(ratio)]
     copies = begin(pairs_io, sems)
     chans = query_ref.shape[0]
@@ -538,17 +550,19 @@
 
     for copy in copies[:7]:
         copy.wait()
-    row_id = lax.broadcasted_iota(jnp.int32, (2 * planes, chans), 0)
-    stack = jnp.concatenate(
-        [jnp.broadcast_to(w_in_ref[c, 1:2].astype(jnp.float32), (wide, chans)) for c in range(6)], axis=0
-    )
-    heads3 = jnp.concatenate(
-        [jnp.broadcast_to(head_ref[c, 1:2].astype(jnp.float32), (wide, chans)) for c in range(3)], axis=0
-    )
+    bf = jnp.bfloat16
+    sub = lax.broadcasted_iota(jnp.int32, (16, chans), 0)
+    blank = jnp.zeros((16, chans), bf)
+    spread_in = [jnp.broadcast_to(w_in_ref[c, 1:2].astype(jnp.float32), (16, chans)) for c in range(6)]
+    spread_head = [jnp.broadcast_to(head_ref[c, 1:2].astype(jnp.float32), (16, chans)) for c in range(3)]
     for w in range(wide):
-        here = lax.rem(row_id, wide) == w
-        inbig[:, w * chans : (w + 1) * chans] = jnp.where(here, stack, 0.0).astype(jnp.bfloat16)
-        headbig[:, w * chans : (w + 1) * chans] = jnp.where(here[:planes], heads3, 0.0).astype(jnp.bfloat16)
+        lanes = slice(w * chans, (w + 1) * chans)
+        here = sub == w % 16
+        for rows_of, big in ((spread_in, inbig), (spread_head, headbig)):
+            for c, row in enumerate(rows_of):
+                one = jnp.where(here, row, 0.0).astype(bf)
+                for n in range(wide // 16):
+                    big[c * wide + 16 * n : c * wide + 16 * (n + 1), lanes] = one if n == w // 16 else blank
     zero_tap = jnp.zeros((chans, chans), jnp.bfloat16)
     for d in range(4):
         for a in range(3):
@@ -705,11 +719,13 @@
 
     def couple(j, carry):
         together(back(2 * j, 0), front(2 * j + 1, 1))
-        together(back(2 * j + 1, 1), front(jnp.minimum(2 * j + 2, total - 1), 0))
+        together(back(2 * j + 1, 1), front(2 * j + 2, 0))
         return carry
 
     together(front(0, 0))
-    lax.fori_loop(0, total // 2, couple, 0)
+    lax.fori_loop(0, total // 2 - 1, couple, 0)
+    together(back(total - 2, 0), front(total - 1, 1))
+    together(back(total - 1, 1))
 
 
 def last_call(ratio, tall, steps, ids, noise, near, far, loads, weights):
@@ -791,11 +807,6 @@
     tall = rows_dev * groups // cols
 
     noise_t = final_noise.swapaxes(3, 4)
-    swaps = [(i, i + 1) for i in range(0, groups - 1, 2)]
-    near = lax.ppermute(noise_t, "space", swaps + [(j, i) for i, j in swaps])
-    swaps = [(i, i + 1) for i in range(1, groups - 1, 2)]
-    far = lax.ppermute(noise_t, "space", swaps + [(j, i) for i, j in swaps])
-
     steps = step_ids.T
     chans_base = base_query.shape[1]
     base_x = base_noise.transpose(1, 2, 0, 3)[0]
@@ -813,7 +824,7 @@
     up_gain = upscale_gain.transpose(1, 0, 2)
     up_head = upscale_head.transpose(2, 0, 1)
     up_w = (up_in, upscale_time, up_gain, upscale_conv, upscale_query, upscale_output, up_head)
-    kv_base, bundle, first_next = front_call(
+    kv_base, bundle, first_next, mine = front_call(
         segments,
         steps,
         token_ids,
@@ -825,6 +836,8 @@
         text_states.reshape(micro * ltxt, dt5),
         base_keyval,
         upscale_keyval,
+        noise_t,
+        ratio,
     )
     duos = ratio // 2
     cross = [
@@ -837,11 +850,16 @@
         for k in range(duos)
     ]
     got = [lax.ppermute(bundle, ("segment", "space"), cross[k]) for k in range(duos)]
+    swaps = [(i, i + 1) for i in range(0, groups - 1, 2)]
+    near = lax.ppermute(mine, "space", swaps + [(j, i) for i, j in swaps])
+    swaps = [(i, i + 1) for i in range(1, groups - 1, 2)]
+    far = lax.ppermute(mine, "space", swaps + [(j, i) for i, j in swaps])
+
     early = base_call(segments, steps, token_ids, base_x, base_w, first_next, kv_base)
     mates = [(i, i ^ 1) for i in range(groups)]
     got, early = lax.optimization_barrier((got, early))
     loads = got + [lax.ppermute(array, "space", mates) for array in got]
-    final = last_call(ratio, tall, steps, token_ids, noise_t, near, far, loads, up_w)
+    final = last_call(ratio, tall, steps, token_ids, mine, near, far, loads, up_w)
     early_states = early.transpose(0, 2, 1, 3)[:, :, None]
     return early_states, final.swapaxes(4, 5)
 

time: 54.6 us -> 54 us (0.989)
  the two profiles are of different devices: /device:TPU:29 before, /device:TPU:1 now
where the time goes in v2:
time: 54 us; the launch traced here: 53.5 us
  Pallas kernels  38.4 us (71%)
  starting transfers between devices  11.1 us (21%)
  waiting for transfers between devices  3.22 us (6%)
  between operations  0.84 us (2%)
    pallas_call x1, Pallas kernels, last_call(): pl.pallas_call(functools.partial(last_kernel, ratio, tall), out_shape=jax...  16.5 us
    pallas_call x1, Pallas kernels, front_call(): pl.pallas_call(front_kernel, out_shape=(jax.ShapeDtypeStruct((rows_text,...  13.2 us
    pallas_call x1, Pallas kernels, base_call(): pl.pallas_call(base_kernel, out_shape=jax.ShapeDtypeStruct((2, 3, micro,...  8.67 us
    ppermute x1, starting transfers between devices, shards(): far = lax.ppermute(mine, 'space', swaps + [(j, i) for i, j in swaps])  8.09 us
    ppermute x1, waiting for transfers between devices, shards(): far = lax.ppermute(mine, 'space', swaps + [(j, i) for i, j in swaps])  3.21 us
    ppermute x1, starting transfers between devices, shards(): lax.ppermute(bundle, ('segment', 'space'), cross[k])  2.83 us
  transfers between devices with their start and end apart: 4, of which 1 were waited for; matrix products, arithmetic and copies ran while one was open for 0% of the time, Pallas kernels for 16%

profile of v2, /device:TPU:1, one launch (start us, length us, event | category | flops | bytes accessed | tf_op | source)
XLA Modules:
  0.0 53.5 jit_solution(628761844594068871)
XLA Ops:
  0.6 13.2 %text_and_first.1 = (bf16[256,1024]{1,0:T(8,128)(2,1)}, bf16[288,256]{1,0:T(8,128)(2,1)}, bf16[3,2,256]{2,1,0:T(2,128)(2,1)}, bf16[2,2,3,32,64]{4,3,2,1,0:T(8,128)(2,1)}) custom-call(s32[2,3]{1,0:T(2,128)} %bitcast.37, bf16[256,4096]{1,0:T(8,128)(2,1)} %bitcast.23, f32[1,4096]{1,0:T(1,128)} %bitcast.25, s32[2,8,128]{2,1,0:T(8,128)} %refs_0_.1, ...), custom_call_target="tpu_custom_call" | custom-call | flops 5000000000 | bytes 22000000 | tf_op jit(solution)/shard_map/text_and_first/pallas_call | solution.py:461
  13.9 2.8 %collective-permute-start = (bf16[288,256]{1,0:T(8,128)(2,1)}, bf16[288,256]{1,0:T(8,128)(2,1)}, u32[]{:S(2)}, u32[]{:S(2)}) collective-permute-start(bf16[288,256]{1,0:T(8,128)(2,1)} %get-tuple-element.8), channel_id=1, source_target_pairs={{0,0},{1,1},{2,8},{3,9},{4,16},{5,17},{6,24},{7,25},{8,2},{9,3},{1... | collective-permute-start | bytes 442376 | tf_op jit(solution)/shard_map/ppermute | solution.py:852
  16.7 8.7 %base_section.1 = bf16[2,3,2,256]{3,2,1,0:T(2,128)(2,1)} custom-call(s32[2,3]{1,0:T(2,128)} %bitcast.38, bf16[3,2,1024]{2,1,0:T(2,128)(2,1)} %bitcast.28, bf16[3,512]{1,0:T(4,128)(2,1)} %refs_1_.1, f32[3,512]{1,0:T(4,128)} %refs_2_.3, bf16[3,512]{1,0:T(4,128)(2,1)} %bitcast.30, bf16[512,512]{1,0:T(8,128)(2,1)} %refs_4_.1, bf16[4608,512]{1,0:T(8,128)(2,1)} %bitcast.22, ...), custom_call_target="tpu_custom_call" | custom-call | flops 4000000000 | bytes 7000000 | tf_op jit(solution)/shard_map/base_section/pallas_call | solution.py:505
  25.4 0.0 collective-permute-done.refs_11_
  25.4 0.1 collective-permute-start.3
  25.5 8.1 %collective-permute-start.2 = (bf16[2,2,3,32,64]{4,3,2,1,0:T(8,128)(2,1)}, bf16[2,2,3,32,64]{4,3,2,1,0:T(8,128)(2,1)}, u32[]{:S(2)}, u32[]{:S(2)}) collective-permute-start(bf16[2,2,3,32,64]{4,3,2,1,0:T(8,128)(2,1)} %get-tuple-element.12.refs_1_), channel_id=1, source_target_pairs={{1,2},{3,4},{5,6},{2,1},{4,3},{6,5},{9,10},{11,12},{13,14},{10,9},... | collective-permute-start | bytes 147464 | tf_op jit(solution)/shard_map/ppermute | solution.py:856
  33.6 0.1 collective-permute-start.1
  33.6 3.2 %collective-permute-done.2.refs_3_ = bf16[2,2,3,32,64]{4,3,2,1,0:T(8,128)(2,1)} collective-permute-done((bf16[2,2,3,32,64]{4,3,2,1,0:T(8,128)(2,1)}, bf16[2,2,3,32,64]{4,3,2,1,0:T(8,128)(2,1)}, u32[]{:S(2)}, u32[]{:S(2)}) %collective-permute-start.2) | collective-permute-done | bytes 49184 | tf_op jit(solution)/shard_map/ppermute | solution.py:856
  36.9 0.0 collective-permute-done.1.refs_2_
  36.9 0.0 collective-permute-done.3.refs_12_
  36.9 16.5 %last_section.1 = bf16[2,2,2,3,32,64]{5,4,3,2,1,0:T(8,128)(2,1)} custom-call(s32[2,3]{1,0:T(2,128)} %bitcast.39, s32[2,8,128]{2,1,0:T(8,128)} %refs_0_.1, bf16[2,2,3,32,64]{4,3,2,1,0:T(8,128)(2,1)} %get-tuple-element.12.refs_1_, bf16[2,2,3,32,64]{4,3,2,1,0:T(8,128)(2,1)} %collective-permute-done.1.refs_2_, ...), custom_call_target="tpu_custom_call" | custom-call | flops 10000000000 | bytes 4000000 | tf_op jit(solution)/shard_map/last_section/pallas_call | solution.py:744
Async XLA Ops:
  13.9 11.5 %collective-permute-start = (bf16[288,256]{1,0:T(8,128)(2,1)}, bf16[288,256]{1,0:T(8,128)(2,1)}, u32[]{:S(2)}, u32[]{:S(2)}) collective-permute-start(bf16[288,256]{1,0:T(8,128)(2,1)} %get-tuple-element.8), channel_id=1, source_target_pairs={{0,0},{1,1},{2,8},{3,9},{4,16},{5,17},{6,24},{7,25},{8,2},{9,3},{1... | collective-permute-start | bytes 442376 | tf_op jit(solution)/shard_map/ppermute | solution.py:852
  25.4 11.5 %collective-permute-start.3 = (bf16[288,256]{1,0:T(8,128)(2,1)}, bf16[288,256]{1,0:T(8,128)(2,1)}, u32[]{:S(2)}, u32[]{:S(2)}) collective-permute-start(bf16[288,256]{1,0:T(8,128)(2,1)} %collective-permute-done.refs_11_), channel_id=1, source_target_pairs={{0,1},{1,0},{2,3},{3,2},{4,5},{5,4},{6,7},{7,6},{8,9},{9,8},{10,11... | collective-permute-start | bytes 442376 | tf_op jit(solution)/shard_map/ppermute | solution.py:861
  25.5 11.4 %collective-permute-start.2 = (bf16[2,2,3,32,64]{4,3,2,1,0:T(8,128)(2,1)}, bf16[2,2,3,32,64]{4,3,2,1,0:T(8,128)(2,1)}, u32[]{:S(2)}, u32[]{:S(2)}) collective-permute-start(bf16[2,2,3,32,64]{4,3,2,1,0:T(8,128)(2,1)} %get-tuple-element.12.refs_1_), channel_id=1, source_target_pairs={{1,2},{3,4},{5,6},{2,1},{4,3},{6,5},{9,10},{11,12},{13,14},{10,9},... | collective-permute-start | bytes 147464 | tf_op jit(solution)/shard_map/ppermute | solution.py:856
  33.6 3.3 %collective-permute-start.1 = (bf16[2,2,3,32,64]{4,3,2,1,0:T(8,128)(2,1)}, bf16[2,2,3,32,64]{4,3,2,1,0:T(8,128)(2,1)}, u32[]{:S(2)}, u32[]{:S(2)}) collective-permute-start(bf16[2,2,3,32,64]{4,3,2,1,0:T(8,128)(2,1)} %get-tuple-element.12.refs_1_), channel_id=1, source_target_pairs={{0,1},{2,3},{4,5},{6,7},{1,0},{3,2},{5,4},{7,6},{8,9},{10,11},{12,... | collective-permute-start | bytes 147464 | tf_op jit(solution)/shard_map/ppermute | solution.py:854

commit v3 on v2

--- a/solution.py
+++ b/solution.py
@@ -251,9 +251,11 @@
         (up_out_hbm.at[0], up_out_ref),
     )
     ratio = mine_out.shape[1]
-    late = ((conv_hbm, conv), (query_hbm, w_query), (out_hbm, w_out))
+    third = 3 * cb
+    late = tuple((conv_hbm.at[a * third : (a + 1) * third], conv.at[a * third : (a + 1) * third]) for a in range(3))
+    late += ((query_hbm, w_query), (out_hbm, w_out))
     late += ((noise_hbm.at[:, pl.ds(seg * ratio, ratio)], mine_out),)
-    copies = begin(list(early) + list(small) + chunks[:n_base] + list(late[:3]) + chunks[n_base:] + list(late[3:]), sems)
+    copies = begin(list(early) + list(small) + chunks[:n_base] + list(late[:5]) + chunks[n_base:] + list(late[5:]), sems)
     first_small = len(early)
     first_chunk = first_small + len(small)
     after = first_chunk + n_base
@@ -314,10 +316,12 @@
     for n in range(n_base):
         copies[first_chunk + n].wait()
         kv_base_out[:, n * step : (n + 1) * step] = (fdot(context[...], kv_w[n]) * scale).astype(bf)
-    copies[after].wait()
-    h1 = jnp.concatenate(corner_h, axis=0) + fdot(taps[...], conv[...])
-    copies[after + 1].wait()
-    copies[after + 2].wait()
+    h1 = jnp.concatenate(corner_h, axis=0)
+    for a in range(3):
+        copies[after + a].wait()
+        h1 = h1 + fdot(taps[:, a * third : (a + 1) * third], conv[a * third : (a + 1) * third])
+    copies[after + 3].wait()
+    copies[after + 4].wait()
     keyvals = [lambda at, m=m: kv_base_out[m * ltxt : (m + 1) * ltxt, at] for m in range(micro)]
     head_rows = [base_head_ref[c : c + 1].astype(f32) for c in range(3)]
     eps = back_part(
@@ -327,7 +331,7 @@
     noise = jnp.concatenate([noise[:, side * h : side * h + quarter] for h in range(quarter)], axis=1)
     corner, _ = denoise(noise, eps, step_ref, 0)
 
-    for copy in copies[after + 3 :]:
+    for copy in copies[after + 5 :]:
         copy.wait()
     rest_kv = (fdot(context[...], kv_w[n_base]) * scale).astype(bf)
     kv_first[...] = rest_kv[:, :half]
@@ -395,7 +399,10 @@
     band = side // segments
     ltxt = kv_ref.shape[0] // micro
     bf, f32 = jnp.bfloat16, jnp.float32
-    copies = begin(list(zip(hbm, vmem)), sems)
+    plan = list(zip(hbm, vmem))
+    third = conv.shape[0] // 3
+    cuts = [tuple(ref.at[a * third : (a + 1) * third] for ref in plan[5]) for a in range(3)]
+    copies = begin(plan[:5] + cuts + plan[6:], sems)
     for copy in copies[:5]:
         copy.wait()
     chans = gain_ref.shape[1]
@@ -409,16 +416,18 @@
     temb = fdot(embed(step_ref, 0, chans), time_ref[...])
     rows = [w_in_ref[c : c + 1].astype(f32) for c in range(3)]
     kept = band * side
-    hid, lhs = [], []
+    hid = []
     for m in range(micro):
         h0 = fdot(x_t, mix_rows(rows, m, micro, 8).astype(bf)) + temb[m : m + 1]
         act = inside_only(silu(unit(h0) * gain_ref[0:1]), side, seg, segments)
         spread_cols(act, side, pad, cols.at[m])
         hid.append(h0[side : side + kept])
-        lhs.append(jnp.concatenate([cols[m, a * side : a * side + kept] for a in range(3)], axis=1))
-    copies[5].wait()
-    h1 = jnp.concatenate(hid, axis=0) + fdot(jnp.concatenate(lhs, axis=0), conv[...])
-    for copy in copies[6:]:
+    h1 = jnp.concatenate(hid, axis=0)
+    for a in range(3):
+        copies[5 + a].wait()
+        lhs = jnp.concatenate([cols[m, a * side : a * side + kept] for m in range(micro)], axis=0)
+        h1 = h1 + fdot(lhs, conv[a * third : (a + 1) * third])
+    for copy in copies[8:]:
         copy.wait()
     biases = [key_bias(ids_ref, m, place) for m in range(micro)]
     keyvals = [lambda at, m=m: kv_ref[m * ltxt : (m + 1) * ltxt, at] for m in range(micro)]
@@ -481,7 +490,7 @@
             pltpu.VMEM((8, near + px + near), f32),
             pltpu.VMEM(((band + 4) * side + 16, cs), f32),
             pltpu.VMEM((micro, (band + 4) * side, 3 * cs), bf),
-            pltpu.SemaphoreType.DMA((chunks + 20,)),
+            pltpu.SemaphoreType.DMA((chunks + 22,)),
         ],
         compiler_params=pltpu.CompilerParams(vmem_limit_bytes=VMEM_ALL),
         cost_estimate=pl.CostEstimate(flops=5 * 10**9, bytes_accessed=22 * 10**6, transcendentals=10**6),
@@ -512,7 +521,7 @@
             pltpu.VMEM((8, near + px + near), f32),
             pltpu.VMEM(((band + 2) * side + 16, cb), f32),
             pltpu.VMEM((micro, (band + 2) * side, 3 * cb), bf),
-            pltpu.SemaphoreType.DMA((len(args),)),
+            pltpu.SemaphoreType.DMA((len(args) + 2,)),
         ],
         compiler_params=pltpu.CompilerParams(vmem_limit_bytes=VMEM_ALL),
         cost_estimate=pl.CostEstimate(flops=4 * 10**9, bytes_accessed=7 * 10**6, transcendentals=10**6),

time: 54 us -> 54.1 us (level)
  no operation moved by 1% of the time
where the time goes in v3:
time: 54.1 us; the launch traced here: 53.6 us
  Pallas kernels  38.1 us (70%)
  starting transfers between devices  11.4 us (21%)
  waiting for transfers between devices  3.22 us (6%)
  between operations  0.83 us (2%)
    pallas_call x1, Pallas kernels, last_call(): pl.pallas_call(functools.partial(last_kernel, ratio, tall), out_shape=jax...  16.5 us
    pallas_call x1, Pallas kernels, front_call(): pl.pallas_call(front_kernel, out_shape=(jax.ShapeDtypeStruct((rows_text,...  13.3 us
    ppermute x1, starting transfers between devices, shards(): far = lax.ppermute(mine, 'space', swaps + [(j, i) for i, j in swaps])  8.45 us
    pallas_call x1, Pallas kernels, base_call(): pl.pallas_call(base_kernel, out_shape=jax.ShapeDtypeStruct((2, 3, micro,...  8.31 us
    ppermute x1, waiting for transfers between devices, shards(): far = lax.ppermute(mine, 'space', swaps + [(j, i) for i, j in swaps])  3.21 us
    ppermute x1, starting transfers between devices, shards(): lax.ppermute(bundle, ('segment', 'space'), cross[k])  2.83 us
  transfers between devices with their start and end apart: 4, of which 1 were waited for; matrix products, arithmetic and copies ran while one was open for 0% of the time, Pallas kernels for 16%

profile of v3, /device:TPU:1, one launch (start us, length us, event | category | flops | bytes accessed | tf_op | source)
XLA Modules:
  0.0 53.6 jit_solution(18064267044779401598)
XLA Ops:
  0.6 13.3 %text_and_first.1 = (bf16[256,1024]{1,0:T(8,128)(2,1)}, bf16[288,256]{1,0:T(8,128)(2,1)}, bf16[3,2,256]{2,1,0:T(2,128)(2,1)}, bf16[2,2,3,32,64]{4,3,2,1,0:T(8,128)(2,1)}) custom-call(s32[2,3]{1,0:T(2,128)} %bitcast.37, bf16[256,4096]{1,0:T(8,128)(2,1)} %bitcast.23, f32[1,4096]{1,0:T(1,128)} %bitcast.25, s32[2,8,128]{2,1,0:T(8,128)} %refs_0_.1, ...), custom_call_target="tpu_custom_call" | custom-call | flops 5000000000 | bytes 22000000 | tf_op jit(solution)/shard_map/text_and_first/pallas_call | solution.py:470
  14.0 2.8 %collective-permute-start = (bf16[288,256]{1,0:T(8,128)(2,1)}, bf16[288,256]{1,0:T(8,128)(2,1)}, u32[]{:S(2)}, u32[]{:S(2)}) collective-permute-start(bf16[288,256]{1,0:T(8,128)(2,1)} %get-tuple-element.8), channel_id=1, source_target_pairs={{0,0},{1,1},{2,8},{3,9},{4,16},{5,17},{6,24},{7,25},{8,2},{9,3},{1... | collective-permute-start | bytes 442376 | tf_op jit(solution)/shard_map/ppermute | solution.py:861
  16.8 8.3 %base_section.1 = bf16[2,3,2,256]{3,2,1,0:T(2,128)(2,1)} custom-call(s32[2,3]{1,0:T(2,128)} %bitcast.38, bf16[3,2,1024]{2,1,0:T(2,128)(2,1)} %bitcast.28, bf16[3,512]{1,0:T(4,128)(2,1)} %refs_1_.1, f32[3,512]{1,0:T(4,128)} %refs_2_.3, bf16[3,512]{1,0:T(4,128)(2,1)} %bitcast.30, bf16[512,512]{1,0:T(8,128)(2,1)} %refs_4_.1, bf16[4608,512]{1,0:T(8,128)(2,1)} %bitcast.22, ...), custom_call_target="tpu_custom_call" | custom-call | flops 4000000000 | bytes 7000000 | tf_op jit(solution)/shard_map/base_section/pallas_call | solution.py:514
  25.1 0.0 collective-permute-done.refs_11_
  25.1 0.1 collective-permute-start.3
  25.2 8.4 %collective-permute-start.2 = (bf16[2,2,3,32,64]{4,3,2,1,0:T(8,128)(2,1)}, bf16[2,2,3,32,64]{4,3,2,1,0:T(8,128)(2,1)}, u32[]{:S(2)}, u32[]{:S(2)}) collective-permute-start(bf16[2,2,3,32,64]{4,3,2,1,0:T(8,128)(2,1)} %get-tuple-element.12.refs_1_), channel_id=1, source_target_pairs={{1,2},{3,4},{5,6},{2,1},{4,3},{6,5},{9,10},{11,12},{13,14},{10,9},... | collective-permute-start | bytes 147464 | tf_op jit(solution)/shard_map/ppermute | solution.py:865
  33.7 0.1 collective-permute-start.1
  33.7 3.2 %collective-permute-done.2.refs_3_ = bf16[2,2,3,32,64]{4,3,2,1,0:T(8,128)(2,1)} collective-permute-done((bf16[2,2,3,32,64]{4,3,2,1,0:T(8,128)(2,1)}, bf16[2,2,3,32,64]{4,3,2,1,0:T(8,128)(2,1)}, u32[]{:S(2)}, u32[]{:S(2)}) %collective-permute-start.2) | collective-permute-done | bytes 49184 | tf_op jit(solution)/shard_map/ppermute | solution.py:865
  36.9 0.0 collective-permute-done.1.refs_2_
  36.9 0.0 collective-permute-done.3.refs_12_
  37.0 16.5 %last_section.1 = bf16[2,2,2,3,32,64]{5,4,3,2,1,0:T(8,128)(2,1)} custom-call(s32[2,3]{1,0:T(2,128)} %bitcast.39, s32[2,8,128]{2,1,0:T(8,128)} %refs_0_.1, bf16[2,2,3,32,64]{4,3,2,1,0:T(8,128)(2,1)} %get-tuple-element.12.refs_1_, bf16[2,2,3,32,64]{4,3,2,1,0:T(8,128)(2,1)} %collective-permute-done.1.refs_2_, ...), custom_call_target="tpu_custom_call" | custom-call | flops 10000000000 | bytes 4000000 | tf_op jit(solution)/shard_map/last_section/pallas_call | solution.py:753
Async XLA Ops:
  14.0 11.1 %collective-permute-start = (bf16[288,256]{1,0:T(8,128)(2,1)}, bf16[288,256]{1,0:T(8,128)(2,1)}, u32[]{:S(2)}, u32[]{:S(2)}) collective-permute-start(bf16[288,256]{1,0:T(8,128)(2,1)} %get-tuple-element.8), channel_id=1, source_target_pairs={{0,0},{1,1},{2,8},{3,9},{4,16},{5,17},{6,24},{7,25},{8,2},{9,3},{1... | collective-permute-start | bytes 442376 | tf_op jit(solution)/shard_map/ppermute | solution.py:861
  25.1 11.8 %collective-permute-start.3 = (bf16[288,256]{1,0:T(8,128)(2,1)}, bf16[288,256]{1,0:T(8,128)(2,1)}, u32[]{:S(2)}, u32[]{:S(2)}) collective-permute-start(bf16[288,256]{1,0:T(8,128)(2,1)} %collective-permute-done.refs_11_), channel_id=1, source_target_pairs={{0,1},{1,0},{2,3},{3,2},{4,5},{5,4},{6,7},{7,6},{8,9},{9,8},{10,11... | collective-permute-start | bytes 442376 | tf_op jit(solution)/shard_map/ppermute | solution.py:870
  25.2 11.7 %collective-permute-start.2 = (bf16[2,2,3,32,64]{4,3,2,1,0:T(8,128)(2,1)}, bf16[2,2,3,32,64]{4,3,2,1,0:T(8,128)(2,1)}, u32[]{:S(2)}, u32[]{:S(2)}) collective-permute-start(bf16[2,2,3,32,64]{4,3,2,1,0:T(8,128)(2,1)} %get-tuple-element.12.refs_1_), channel_id=1, source_target_pairs={{1,2},{3,4},{5,6},{2,1},{4,3},{6,5},{9,10},{11,12},{13,14},{10,9},... | collective-permute-start | bytes 147464 | tf_op jit(solution)/shard_map/ppermute | solution.py:865
  33.7 3.3 %collective-permute-start.1 = (bf16[2,2,3,32,64]{4,3,2,1,0:T(8,128)(2,1)}, bf16[2,2,3,32,64]{4,3,2,1,0:T(8,128)(2,1)}, u32[]{:S(2)}, u32[]{:S(2)}) collective-permute-start(bf16[2,2,3,32,64]{4,3,2,1,0:T(8,128)(2,1)} %get-tuple-element.12.refs_1_), channel_id=1, source_target_pairs={{0,1},{2,3},{4,5},{6,7},{1,0},{3,2},{5,4},{7,6},{8,9},{10,11},{12,... | collective-permute-start | bytes 147464 | tf_op jit(solution)/shard_map/ppermute | solution.py:863
